TPU v7x, 32 devices: a whole 2x2x4 slice. The times are simulated.
32 devices in a mesh: shard: 8 (over z, core), replica: 4 (over y, x).
Axes of the slice: x: 2, y: 2, z: 4, core: 2. Of those that a mesh axis runs over, the one named last changes fastest.
Arguments:
- block_in: bfloat16 [4, 1024, 2048], P('replica', 'shard'), may hold values from -6 to 6
- norm_gain: bfloat16 [2048], P('shard'), may hold values from 0.099609375 to 1.8984375
- norm_bias: bfloat16 [2048], P('shard'), may hold values from -3 to 3
- attn_weight: bfloat16 [2048, 6144], P('shard'), may hold values from -0.125 to 0.125
- attn_bias: bfloat16 [6144], P('shard'), may hold values from -3 to 3
- dense_weight: bfloat16 [2048, 2048], P('shard'), may hold values from -0.5 to 0.5
- dense_bias: bfloat16 [2048], P('shard'), may hold values from -3 to 3
- up_weight: bfloat16 [2048, 8192], P('shard'), may hold values from -0.125 to 0.125
- up_bias: bfloat16 [8192], P('shard'), may hold values from -3 to 3
- down_weight: bfloat16 [8192, 2048], P('shard'), may hold values from -0.0625 to 0.0625
- down_bias: bfloat16 [2048], P('shard'), may hold values from -3 to 3
- cotangent: bfloat16 [4, 1024, 2048], P('replica', 'shard'), may hold values from -6 to 6
Outputs:
- block_out: bfloat16 [4, 1024, 2048], P('replica', 'shard')
- grad_in: bfloat16 [4, 1024, 2048], P('replica', 'shard')
- grad_norm_gain: float32 [2048], P('shard')
- grad_norm_bias: float32 [2048], P('shard')
- grad_attn_weight: float32 [2048, 6144], P('shard')
- grad_attn_bias: float32 [6144], P('shard')
- grad_dense_weight: float32 [2048, 2048], P('shard')
- grad_dense_bias: float32 [2048], P('shard')
- grad_up_weight: float32 [2048, 8192], P('shard')
- grad_up_bias: float32 [8192], P('shard')
- grad_down_weight: float32 [8192, 2048], P('shard')
- grad_down_bias: float32 [2048], P('shard')
All inputs are finite; a program needn't handle non-finite values.
Results may differ from a plain program's by a relative error of at most 0.018.
Values may be sent and summed in bfloat16 or wider, within the bound.
No kernel may reach another device: no remote copies, remote signals or barrier semaphores. Data moves between devices by JAX's collectives and lax.ppermute only.
A program may use at most 704 MiB of HBM per device.

v0:
```python
import math

import jax
import jax.numpy as jnp
from jax import lax
from jax.sharding import PartitionSpec as P

D = 2048
H = 32
HD = 64
ROT = 32
FF = 8192


EPSILON = 1e-05
ROPE_BASE = 10000.0
MASK_VALUE = -1e30


def layer_norm(values, norm_gain, norm_shift):
    center = values - jnp.mean(values, axis=-1, keepdims=True)
    spread = jnp.mean(center * center, axis=-1, keepdims=True)
    return center * lax.rsqrt(spread + EPSILON) * norm_gain + norm_shift


def rotate(values, positions):
    half_rot = ROT // 2
    frequencies = ROPE_BASE ** (-2.0 * jnp.arange(half_rot, dtype=jnp.float32) / ROT)
    angles = positions[:, None] * frequencies[None, :]
    cosine_rows = jnp.cos(angles)[:, None, :]
    sine_rows = jnp.sin(angles)[:, None, :]
    first_half = values[..., :half_rot]
    second_half = values[..., half_rot:ROT]
    return jnp.concatenate(
        [
            first_half * cosine_rows - second_half * sine_rows,
            second_half * cosine_rows + first_half * sine_rows,
            values[..., ROT:],
        ],
        axis=-1,
    )


def gelu_tanh(values):
    return jax.nn.gelu(values, approximate=True)


def dot_last(left, right):
    return lax.dot_general(
        left, right, (((1,), (1,)), ((), ())), preferred_element_type=jnp.float32
    )


def dot_first(left, right):
    return lax.dot_general(
        left, right, (((0,), (0,)), ((), ())), preferred_element_type=jnp.float32
    )


def pack_small(norm_gain, norm_bias, attn_bias, dense_bias, up_bias, down_bias):
    row_count = norm_gain.shape[0]
    fc2_ratio = FF // D
    return jnp.concatenate(
        [
            norm_gain[:, None],
            norm_bias[:, None],
            attn_bias.reshape(row_count, 3),
            dense_bias[:, None],
            up_bias.reshape(row_count, fc2_ratio),
            down_bias[:, None],
        ],
        axis=1,
    )


def unpack_small(gathered):
    fc2_ratio = FF // D
    gathered = gathered.astype(jnp.float32)
    return (
        gathered[:, 0],
        gathered[:, 1],
        gathered[:, 2:5].reshape(-1),
        gathered[:, 5],
        gathered[:, 6 : 6 + fc2_ratio].reshape(-1),
        gathered[:, 6 + fc2_ratio],
    )


def shards(
    block_in,
    norm_gain,
    norm_bias,
    attn_weight,
    attn_bias,
    dense_weight,
    dense_bias,
    up_weight,
    up_bias,
    down_weight,
    down_bias,
    cotangent,
):
    fc2_ratio = FF // D
    tok_rows = block_in.shape[1]
    shard_count = lax.axis_size("shard")
    shard_index = lax.axis_index("shard")
    seq_len = tok_rows * shard_count
    local_rows = attn_weight.shape[0]
    inputs = block_in[0].astype(jnp.float32)
    down_rows = down_weight.reshape(local_rows, fc2_ratio * D)
    packed = pack_small(norm_gain, norm_bias, attn_bias, dense_bias, up_bias, down_bias)
    whole_small = lax.all_gather(packed, "shard", axis=0, tiled=True)
    gain_full, shift_full, attn_bias_full, dense_bias_full, up_bias_full, down_bias_full = (
        unpack_small(whole_small)
    )
    normed = layer_norm(inputs, gain_full, shift_full).astype(jnp.bfloat16)
    pieces = (
        lax.all_gather(attn_weight, "shard", axis=0, tiled=True),
        lax.all_gather(up_weight, "shard", axis=0, tiled=True),
    )
    projected = jnp.dot(normed, pieces[0], preferred_element_type=jnp.float32)
    hidden_pre = jnp.dot(normed, pieces[1], preferred_element_type=jnp.float32)
    projected = projected + attn_bias_full
    hidden_pre = hidden_pre + up_bias_full
    query_pos = shard_index * tok_rows + jnp.arange(tok_rows, dtype=jnp.int32)
    positions = query_pos.astype(jnp.float32)
    queries = projected[:, :D].reshape(tok_rows, H, HD)
    keys_local = projected[:, D : 2 * D].reshape(tok_rows, H, HD)
    values_local = projected[:, 2 * D :].astype(jnp.bfloat16)
    rot_queries = rotate(queries, positions).astype(jnp.bfloat16)
    rot_keys = rotate(keys_local, positions).astype(jnp.bfloat16).reshape(tok_rows, D)
    all_keys, all_values = (
        lax.all_gather(rot_keys, "shard", axis=0, tiled=True),
        lax.all_gather(values_local, "shard", axis=0, tiled=True),
    )
    key_block = math.gcd(seq_len, 512)
    needed = ((shard_index + 1) * tok_rows + key_block - 1) // key_block
    score_scale = HD ** (-0.5)

    def block_scores(block_index):
        key_rows = lax.dynamic_slice_in_dim(
            all_keys, block_index * key_block, key_block, 0
        ).reshape(key_block, H, HD)
        value_rows = lax.dynamic_slice_in_dim(
            all_values, block_index * key_block, key_block, 0
        ).reshape(key_block, H, HD)
        scores = (
            jnp.einsum("qhd,khd->hqk", rot_queries, key_rows, preferred_element_type=jnp.float32)
            * score_scale
        )
        key_pos = block_index * key_block + jnp.arange(key_block, dtype=jnp.int32)
        allowed = key_pos[None, :] <= query_pos[:, None]
        return (jnp.where(allowed[None], scores, MASK_VALUE), key_rows, value_rows)

    def running_max(block_index, loop_state):
        row_max, row_total = loop_state
        scores, key_rows, value_rows = block_scores(block_index)
        new_max = jnp.maximum(row_max, jnp.max(scores, axis=-1))
        row_total = row_total * jnp.exp(row_max - new_max) + jnp.sum(
            jnp.exp(scores - new_max[..., None]), axis=-1
        )
        return (new_max, row_total)

    row_max, row_total = lax.fori_loop(
        0,
        needed,
        running_max,
        (jnp.full((H, tok_rows), MASK_VALUE, jnp.float32), jnp.zeros((H, tok_rows), jnp.float32)),
    )
    log_total = row_max + jnp.log(row_total)

    def weighted_sum(block_index, accumulated):
        scores, key_rows, value_rows = block_scores(block_index)
        weights = jnp.exp(scores - log_total[..., None]).astype(jnp.bfloat16)
        return accumulated + jnp.einsum(
            "hqk,khd->qhd", weights, value_rows, preferred_element_type=jnp.float32
        )

    mixed_rows = lax.fori_loop(0, needed, weighted_sum, jnp.zeros((tok_rows, H, HD), jnp.float32))
    mixed_low = mixed_rows.reshape(tok_rows, D).astype(jnp.bfloat16)
    hidden = gelu_tanh(hidden_pre).astype(jnp.bfloat16)
    pieces = (
        lax.all_gather(dense_weight, "shard", axis=0, tiled=True),
        lax.all_gather(down_rows, "shard", axis=0, tiled=True),
    )
    row_count = pieces[0].shape[0]
    branches = jnp.dot(mixed_low, pieces[0], preferred_element_type=jnp.float32) + jnp.dot(
        hidden, pieces[1].reshape(row_count * fc2_ratio, D), preferred_element_type=jnp.float32
    )
    block_out = (inputs + branches + dense_bias_full + down_bias_full).astype(jnp.bfloat16)[None]
    upstream = cotangent[0]
    pieces = (
        lax.all_gather(dense_weight, "shard", axis=0, tiled=True),
        lax.all_gather(down_rows, "shard", axis=0, tiled=True),
    )
    row_count = pieces[0].shape[0]
    part_attn = dot_last(upstream, pieces[0])
    part_mlp = dot_last(upstream, pieces[1].reshape(row_count * fc2_ratio, D))
    grad_mixed_low = part_attn.astype(jnp.bfloat16)
    unused_value, gelu_back = jax.vjp(gelu_tanh, hidden_pre)
    grad_pre = gelu_back(part_mlp)[0].astype(jnp.bfloat16)
    grad_heads = grad_mixed_low.reshape(tok_rows, H, HD)
    row_delta = jnp.sum(grad_heads.astype(jnp.float32) * mixed_rows, axis=-1).T

    def score_grads(block_index):
        scores, key_rows, value_rows = block_scores(block_index)
        prob_rows = jnp.exp(scores - log_total[..., None])
        weights = prob_rows.astype(jnp.bfloat16)
        grad_probs = jnp.einsum(
            "qhd,khd->hqk", grad_heads, value_rows, preferred_element_type=jnp.float32
        )
        grad_scores = (prob_rows * (grad_probs - row_delta[..., None])).astype(jnp.bfloat16)
        return (grad_scores, weights, key_rows)

    def backward_block(block_index, loop_state):
        grad_queries, key_grads = loop_state
        grad_scores, weights, key_rows = score_grads(block_index)
        grad_queries = grad_queries + jnp.einsum(
            "hqk,khd->qhd", grad_scores, key_rows, preferred_element_type=jnp.float32
        )
        grad_keys = (
            jnp.einsum("hqk,qhd->khd", grad_scores, rot_queries, preferred_element_type=jnp.float32)
            * score_scale
        )
        grad_values = jnp.einsum(
            "hqk,qhd->khd", weights, grad_heads, preferred_element_type=jnp.float32
        )
        rows_out = jnp.concatenate(
            [grad_keys.reshape(key_block, D), grad_values.reshape(key_block, D)], axis=1
        )
        key_grads = lax.dynamic_update_slice(
            key_grads, rows_out, (block_index * key_block, jnp.int32(0))
        )
        return (grad_queries, key_grads)

    grad_queries, key_grads = lax.fori_loop(
        0,
        needed,
        backward_block,
        (jnp.zeros((tok_rows, H, HD), jnp.float32), jnp.zeros((seq_len, 2 * D), jnp.float32)),
    )
    own_grads = lax.psum_scatter(
        key_grads.astype(jnp.bfloat16), "shard", scatter_dimension=0, tiled=True
    ).astype(jnp.float32)
    grad_keys_own = own_grads[:, :D].reshape(tok_rows, H, HD)
    grad_values_own = own_grads[:, D:]
    grad_queries = grad_queries * score_scale

    def rotate_pair(query_heads, key_heads):
        return (rotate(query_heads, positions), rotate(key_heads, positions))

    unused_pair, rope_back = jax.vjp(rotate_pair, queries, keys_local)
    grad_query_pre, grad_key_pre = rope_back((grad_queries, grad_keys_own))
    grad_projected = jnp.concatenate(
        [grad_query_pre.reshape(tok_rows, D), grad_key_pre.reshape(tok_rows, D), grad_values_own],
        axis=1,
    ).astype(jnp.bfloat16)
    pieces = (
        lax.all_gather(attn_weight, "shard", axis=0, tiled=True),
        lax.all_gather(up_weight, "shard", axis=0, tiled=True),
    )
    part_rows = dot_last(grad_projected, pieces[0]) + dot_last(grad_pre, pieces[1])
    unused_norm, norm_back = jax.vjp(layer_norm, inputs, gain_full, shift_full)
    grad_inputs, grad_gain, grad_shift = norm_back(part_rows)
    grad_in = (upstream.astype(jnp.float32) + grad_inputs).astype(jnp.bfloat16)[None]
    grad_bias_attn = jnp.sum(grad_projected.astype(jnp.float32), axis=0)
    grad_bias_up = jnp.sum(grad_pre.astype(jnp.float32), axis=0)
    grad_bias_out = jnp.sum(upstream.astype(jnp.float32), axis=0)
    small_cols = jnp.concatenate(
        [
            grad_gain[:, None],
            grad_shift[:, None],
            grad_bias_attn.reshape(D, 3),
            grad_bias_out[:, None],
            grad_bias_up.reshape(D, fc2_ratio),
            grad_bias_out[:, None],
            jnp.zeros((D, 121 - fc2_ratio), jnp.float32),
        ],
        axis=1,
    )
    own_rows = lax.psum_scatter(
        jnp.concatenate(
            [
                dot_first(normed, grad_projected),
                dot_first(normed, grad_pre),
                dot_first(mixed_low, upstream),
                dot_first(hidden, upstream).reshape(
                    local_rows * lax.axis_size("shard"), fc2_ratio * D
                ),
                small_cols,
            ],
            axis=1,
        ).astype(jnp.bfloat16),
        "shard",
        scatter_dimension=0,
        tiled=True,
    )
    summed = lax.psum(own_rows, "replica").astype(jnp.float32)
    base_col = 4 * D + 2 * FF
    grad_attn_weight = summed[:, : 3 * D]
    grad_up_weight = summed[:, 3 * D : 3 * D + FF]
    grad_dense_weight = summed[:, 3 * D + FF : 4 * D + FF]
    grad_down_weight = summed[:, 4 * D + FF : base_col].reshape(local_rows * fc2_ratio, D)
    grad_norm_gain = summed[:, base_col]
    grad_norm_bias = summed[:, base_col + 1]
    grad_attn_bias = summed[:, base_col + 2 : base_col + 5].reshape(-1)
    grad_dense_bias = summed[:, base_col + 5]
    grad_up_bias = summed[:, base_col + 6 : base_col + 6 + fc2_ratio].reshape(-1)
    grad_down_bias = summed[:, base_col + 6 + fc2_ratio]
    return (
        block_out,
        grad_in,
        grad_norm_gain,
        grad_norm_bias,
        grad_attn_weight,
        grad_attn_bias,
        grad_dense_weight,
        grad_dense_bias,
        grad_up_weight,
        grad_up_bias,
        grad_down_weight,
        grad_down_bias,
    )


def solution(mesh):
    return jax.shard_map(
        shards,
        mesh=mesh,
        in_specs=(
            P("replica", "shard", None),
            P("shard"),
            P("shard"),
            P("shard", None),
            P("shard"),
            P("shard", None),
            P("shard"),
            P("shard", None),
            P("shard"),
            P("shard", None),
            P("shard"),
            P("replica", "shard", None),
        ),
        out_specs=(
            P("replica", "shard", None),
            P("replica", "shard", None),
            P("shard"),
            P("shard"),
            P("shard", None),
            P("shard"),
            P("shard", None),
            P("shard"),
            P("shard", None),
            P("shard"),
            P("shard", None),
            P("shard"),
        ),
        check_vma=False,
    )
```

profile of v0, /device:TPU:0, one launch (start us, length us, event | category | flops | bytes accessed | tf_op | source)
XLA Modules:
  0.0 2586.5 jit_solution(3046557154003619695)
XLA Ops:
  9.6 15.6 all_gather.25
  27.9 204.4 %all-gather.7.cloned.1.call-done = bf16[2048,6144]{1,0:T(8,128)(2,1)} async-done(((bf16[256,6144]{1,0:T(8,128)(2,1)}), bf16[2048,6144]{1,0:T(8,128)(2,1)}) %all-gather.7.cloned.1.call-update) | async-done | bytes 25165840 | tf_op jit(solution)/shard_map/all_gather | solution.py:118
  232.3 10.8 convolution_add_fusion.1
  243.2 1.7 copy-done.5
  245.9 1.7 fusion.81
  249.4 8.0 reshape.302
  258.1 56.1 %all-gather.13.cloned.1.call-done = bf16[2048,2048]{1,0:T(8,128)(2,1)} async-done(((bf16[256,2048]{1,0:T(8,128)(2,1)}), bf16[2048,2048]{1,0:T(8,128)(2,1)}) %all-gather.13.cloned.1.call-update) | async-done | bytes 8388624 | tf_op jit(solution)/shard_map/all_gather | solution.py:183
  314.2 6.3 convolution_convert_fusion.4
  321.6 40.5 %all-gather.9.cloned.1.call-done = bf16[1024,2048]{1,0:T(8,128)(2,1)} async-done(((bf16[128,2048]{1,0:T(8,128)(2,1)}), bf16[1024,2048]{1,0:T(8,128)(2,1)}) %all-gather.9.cloned.1.call-update) | async-done | bytes 4194320 | tf_op jit(solution)/shard_map/all_gather | solution.py:134
  362.1 6.4 copy.69
  368.5 42.2 %all-gather.11.cloned.1.call-done = bf16[1024,2048]{0,1:T(8,128)(2,1)} async-done(((bf16[128,2048]{0,1:T(8,128)(2,1)}), bf16[1024,2048]{0,1:T(8,128)(2,1)}) %all-gather.11.cloned.1.call-update) | async-done | bytes 4194320 | tf_op jit(solution)/shard_map/all_gather | solution.py:133
  410.7 6.1 while.37
  411.3 1.7 constant_dynamic-slice_fusion.8
  413.1 1.9 fusion.137
  415.0 1.7 exponential_reduce_fusion.2
  416.8 1.1 broadcast.210.clone
  417.9 10.9 while.38
  418.0 4.6 constant_dynamic-slice_fusion.9
  422.6 6.2 fusion.142
  428.8 2.0 multiply_reduce_fusion
  431.0 4.5 broadcast_in_dim.116
  435.4 15.3 while.39
  435.8 2.6 constant_dynamic-slice_fusion.10
  438.3 1.3 fusion.153
  439.7 3.4 fusion.154
  443.1 2.4 fusion.156
  445.5 1.3 fusion.155
  446.8 1.6 convolution_multiply_fusion.2
  448.4 2.3 maximum_dynamic-update-slice_fusion.2
  450.7 11.9 copy.83
  464.2 1.3 copy.70
  465.5 1.8 add.200
  469.4 5.7 convolution_convert_fusion.3
  475.1 223.9 %all-gather.17.cloned.1.call-done = bf16[2048,8192]{1,0:T(8,128)(2,1)} async-done(((bf16[256,8192]{1,0:T(8,128)(2,1)}), bf16[2048,8192]{1,0:T(8,128)(2,1)}) %all-gather.17.cloned.1.call-update) | async-done | bytes 33554448 | tf_op jit(solution)/shard_map/all_gather | solution.py:184
  699.0 56.1 %reshape.303 = bf16[8192,2048]{1,0:T(8,128)(2,1)} reshape(bf16[2048,8192]{1,0:T(8,128)(2,1)} %all-gather.17.cloned.1.call-done) | data formatting | bytes 67108864 | tf_op jit(solution)/shard_map/reshape | solution.py:188
  755.2 232.2 %all-gather.15.cloned.1.call-done = bf16[2048,8192]{1,0:T(8,128)(2,1)} async-done(((bf16[256,8192]{1,0:T(8,128)(2,1)}), bf16[2048,8192]{1,0:T(8,128)(2,1)}) %all-gather.15.cloned.1.call-update) | async-done | bytes 33554448 | tf_op jit(solution)/shard_map/all_gather | solution.py:119
  987.4 18.0 convolution_add_fusion
  1005.3 19.1 fusion.84
  1024.5 1.9 reshape.311
  1026.4 16.2 convolution_convert_fusion.1
  1042.6 55.8 %reshape.309 = bf16[2048,8192]{1,0:T(8,128)(2,1)} reshape(bf16[8192,2048]{1,0:T(8,128)(2,1)} %convolution_convert_fusion.1) | data formatting | bytes 67108864 | tf_op jit(solution)/shard_map/reshape | solution.py:287
  1098.4 14.1 convolution_convert_fusion
  1112.5 2.3 fusion.82
  1114.8 2.1 copy.85
  1116.9 1.8 split.27
  1118.7 2.1 convert.92
  1120.8 2.0 copy.86
  1122.9 1.4 multiply_add_fusion.4
  1124.2 1.5 add_convert_fusion.1
  1127.2 13.3 convolution_convert_fusion.2
  1140.5 14.2 fusion.73
  1154.7 17.6 fusion.79
  1173.3 1.7 fusion.60
  1175.8 162.3 %concatenate.26 = bf16[2048,24704]{1,0:T(8,128)(2,1)} concatenate(bf16[2048,6144]{1,0:T(8,128)(2,1)} %convolution_convert_fusion.2, bf16[2048,8192]{1,0:T(8,128)(2,1)} %convolution_convert_fusion, bf16[2048,2048]{1,0:T(8,128)(2,1)} %convolution_convert_fusion.3, bf16[2048,8192]{1,0:T(8,128)(2,1)} %reshape.309, bf16[2048,1]{1,0:T(8,128)(2,1)S(1)} %broadcast_in_dim.130, ...), dimensions={1} | concatenate | bytes 202375168 | tf_op jit(solution)/shard_map/concatenate | solution.py:282
  1338.2 958.2 %reduce-scatter.9.cloned.1.call-done = bf16[256,24704]{1,0:T(8,128)(2,1)} async-done(((bf16[2048,24704]{1,0:T(8,128)(2,1)}), bf16[256,24704]{1,0:T(8,128)(2,1)}) %reduce-scatter.9.cloned.1.call-update) | async-done | bytes 12648464
  2297.4 4.7 fusion.86
  2302.2 19.4 fusion.50
  2321.6 1.2 fusion.63
  2322.8 216.3 %all-reduce.9.cloned.1.call-done = bf16[256,24704]{1,0:T(8,128)(2,1)} async-done(((bf16[256,24704]{1,0:T(8,128)(2,1)}), bf16[256,24704]{1,0:T(8,128)(2,1)}) %all-reduce.9.cloned.1.call-update) | async-done | bytes 12648464 | tf_op jit(solution)/shard_map/psum | solution.py:298
  2542.5 11.8 fusion.80
  2554.3 9.8 reshape.314
  2564.1 6.6 convert_element_type.97
  2571.6 2.8 slice.134
  2574.4 5.3 slice.132
  (158 shorter events, 22.2 us)
Async XLA Ops:
  7.2 1.6 copy-start.35
  7.2 1.6 copy-start.36
  7.2 1.6 copy-start.37
  7.2 1.6 copy-start.38
  7.2 1.7 copy-start.31
  7.2 2.0 copy-start.32
  7.2 19.0 copy-start
  7.3 225.1 %all-gather.7.cloned.1.call-start = ((), (), s32[]{:S(2)}) async-start(), calls=%async_computation.2 | async-start | bytes 28311552 | tf_op jit(solution)/shard_map/all_gather | solution.py:118
  8.0 306.2 %all-gather.13.cloned.1.call-start = ((), (), s32[]{:S(2)}) async-start(), calls=%async_computation.5 | async-start | bytes 9437184 | tf_op jit(solution)/shard_map/all_gather | solution.py:183
  8.7 353.4 %all-gather.9.cloned.1.call-start = ((), (), s32[]{:S(2)}) async-start(), calls=%async_computation.3 | async-start | bytes 4718592 | tf_op jit(solution)/shard_map/all_gather | solution.py:134
  25.2 217.9 %copy-start.19 = (bf16[2048,11]{0,1:T(8,128)(2,1)}, bf16[2048,11]{0,1:T(8,128)(2,1)S(1)}, u32[]{:S(2)}) copy-start(bf16[2048,11]{0,1:T(8,128)(2,1)S(1)} %all_gather.25) | copy-start | bytes 135172
  26.4 216.7 %copy-start.21 = (f32[128]{0:T(128)}, f32[128]{0:T(128)S(1)}, u32[]{:S(2)}) copy-start(f32[128]{0:T(128)S(1)} %broadcast_multiply_fusion.1) | copy-start | bytes 1540
  26.7 0.5 copy-start.33
  27.3 215.8 %copy-start.23 = (f32[128]{0:T(128)}, f32[128]{0:T(128)S(1)}, u32[]{:S(2)}) copy-start(f32[128]{0:T(128)S(1)} %fusion.71) | copy-start | bytes 1540
  27.9 215.2 %copy-start.15 = (f32[2048,1]{0,1:T(1,128)}, f32[2048,1]{0,1:T(1,128)S(1)}, u32[]{:S(2)}) copy-start(f32[2048,1]{0,1:T(1,128)S(1)} %get-tuple-element.363) | copy-start | bytes 24580
  27.9 215.2 %copy-start.17 = (f32[2048,1]{0,1:T(1,128)}, f32[2048,1]{0,1:T(1,128)S(1)}, u32[]{:S(2)}) copy-start(f32[2048,1]{0,1:T(1,128)S(1)} %get-tuple-element.364) | copy-start | bytes 24580
  243.1 1.7 copy-start.5
  245.7 165.0 %all-gather.11.cloned.1.call-start = ((), (), s32[]{:S(2)}) async-start(), calls=%async_computation.4 | async-start | bytes 4718592 | tf_op jit(solution)/shard_map/all_gather | solution.py:133
  245.9 2.4 copy-start.25
  245.9 2.4 copy-start.27
  249.4 449.6 %all-gather.17.cloned.1.call-start = ((), (), s32[]{:S(2)}) async-start(), calls=%async_computation.7 | async-start | bytes 37748736 | tf_op jit(solution)/shard_map/all_gather | solution.py:184
  257.5 56.7 %copy-start.2 = (bf16[1,128,2048]{2,1,0:T(8,128)(2,1)S(1)}, bf16[1,128,2048]{2,1,0:T(8,128)(2,1)}, u32[]{:S(2)}) copy-start(bf16[1,128,2048]{2,1,0:T(8,128)(2,1)} %param.29) | copy-start | bytes 1572868
  257.5 729.8 %all-gather.15.cloned.1.call-start = ((), (), s32[]{:S(2)}) async-start(), calls=%async_computation.6 | async-start | bytes 37748736 | tf_op jit(solution)/shard_map/all_gather | solution.py:119
  258.1 854.4 %reduce-scatter.7.cloned.1.call-start = ((), (), s32[]{:S(2)}) async-start(), calls=%async_computation.9 | async-start | bytes 9437184
  417.9 10.9 copy-start.14
  430.8 38.5 %copy-start.8 = (bf16[128,32,64]{0,2,1:T(8,128)(2,1)}, bf16[128,32,64]{0,2,1:T(8,128)(2,1)S(1)}, u32[]{:S(2)}) copy-start(bf16[128,32,64]{0,2,1:T(8,128)(2,1)S(1)} %get-tuple-element.360) | copy-start | bytes 1572868
  462.6 0.8 copy-start.20
  462.6 1.1 copy-start.3
  462.7 1833.7 %reduce-scatter.9.cloned.1.call-start = ((), (), s32[]{:S(2)}) async-start(), calls=%async_computation.10 | async-start | bytes 113836032
  467.4 1.1 copy-start.13
  475.1 512.3 %copy-start.1 = (bf16[1,128,2048]{2,1,0:T(8,128)(2,1)S(1)}, bf16[1,128,2048]{2,1,0:T(8,128)(2,1)}, u32[]{:S(2)}) copy-start(bf16[1,128,2048]{2,1,0:T(8,128)(2,1)} %param.18) | copy-start | bytes 1572868
  475.1 512.3 %copy-start.16 = (f32[2048,1]{0,1:T(1,128)S(1)}, f32[2048,1]{0,1:T(1,128)}, u32[]{:S(2)}) copy-start(f32[2048,1]{0,1:T(1,128)} %copy-done.15) | copy-start | bytes 24580
  475.1 512.3 %copy-start.18 = (f32[2048,1]{0,1:T(1,128)S(1)}, f32[2048,1]{0,1:T(1,128)}, u32[]{:S(2)}) copy-start(f32[2048,1]{0,1:T(1,128)} %copy-done.17) | copy-start | bytes 24580
  475.1 512.3 %copy-start.22 = (f32[128]{0:T(128)S(1)}, f32[128]{0:T(128)}, u32[]{:S(2)}) copy-start(f32[128]{0:T(128)} %copy-done.21) | copy-start | bytes 1540
  475.1 512.3 %copy-start.24 = (f32[128]{0:T(128)S(1)}, f32[128]{0:T(128)}, u32[]{:S(2)}) copy-start(f32[128]{0:T(128)} %copy-done.23) | copy-start | bytes 1540
  1042.6 55.8 %copy-start.6 = (bf16[128,8192]{1,0:T(8,128)(2,1)S(1)}, bf16[128,8192]{1,0:T(8,128)(2,1)}, u32[]{:S(2)}) copy-start(bf16[128,8192]{1,0:T(8,128)(2,1)} %get-tuple-element.373) | copy-start | bytes 6291460
  1112.5 10.4 copy-start.26
  1112.5 10.4 copy-start.28
  1122.9 3.9 copy-start.10
  1125.7 0.8 copy-start.11
  1125.7 1.0 copy-start.12
  1154.7 17.6 copy-start.34
  1338.1 1201.0 %all-reduce.9.cloned.1.call-start = ((), (), s32[]{:S(2)}) async-start(), calls=%async_computation.8 | async-start | bytes 25296896 | tf_op jit(solution)/shard_map/psum | solution.py:298
  2296.4 1.0 copy-start.9
  2297.4 4.7 copy-start.29
  2297.4 4.7 copy-start.30
  2302.1 19.5 copy-start.4
  2302.1 19.4 copy-start.7
Sparse Core Ops, SparseCore 0:
  9.7 222.5 all-gather.6
  233.9 80.2 all-gather.12
  316.4 45.6 all-gather.8
  364.1 46.5 all-gather.10
  412.1 286.8 all-gather.16
  700.5 286.8 all-gather.14
  990.2 87.7 reduce-scatter.6
  1338.2 958.0 reduce-scatter.8
  2299.9 239.2 all-reduce.8
where the time goes:
time: 2600 us; the launch traced here: 2590 us
  waiting for transfers between devices  1980 us (76%)
  local copies, waits for them, and re-layouts  378 us (15%)
  matrix products  178 us (7%)
    unnamed x11, waiting for transfers between devices  960 us
    all_gather x1, waiting for transfers between devices, shards(): lax.all_gather(up_weight, 'shard', axis=0, tiled=True)  232 us
    all_gather x1, waiting for transfers between devices, shards(): lax.all_gather(down_rows, 'shard', axis=0, tiled=True)  224 us
    psum x1, waiting for transfers between devices, shards(): summed = lax.psum(own_rows, 'replica').astype(jnp.float32)  216 us
    all_gather x1, waiting for transfers between devices, shards(): lax.all_gather(attn_weight, 'shard', axis=0, tiled=True)  204 us
    concatenate x1, local copies, waits for them, and re-layouts, shards(): jnp.concatenate([dot_first(normed, grad_projected), dot_first(normed, gra...  162 us
    dot_general x4, matrix products, dot_last(): lax.dot_general(left, right, (((1,), (1,)), ((), ())), preferred_element_...  57.2 us
    reshape x1, local copies, waits for them, and re-layouts, shards(): pieces[1].reshape(row_count * fc2_ratio, D)  56.1 us
  transfers between devices with their start and end apart: 9, of which 8 were waited for; matrix products, arithmetic and copies ran while one was open for 12% of the time, Pallas kernels for 0%

commit v1 on v0

v1 whole, which is shorter than its diff:
```python
import functools

import jax
import jax.numpy as jnp
from jax import lax
from jax.experimental import pallas as pl
from jax.experimental.pallas import tpu as pltpu
from jax.sharding import PartitionSpec as P

D = 2048
H = 32
HD = 64
ROT = 32
FF = 8192

EPSILON = 1e-05
ROPE_BASE = 10000.0
MASK_VALUE = -1e30
F32 = jnp.float32
BF16 = jnp.bfloat16
GELU_C = 0.7978845608028654


def dot(left, right, contract=(1, 0)):
    return lax.dot_general(
        left, right, (((contract[0],), (contract[1],)), ((), ())), preferred_element_type=F32
    )


def chip_shift(shard_count, k):
    chips = shard_count // 2
    return [(2 * z + c, 2 * ((z + k) % chips) + c) for z in range(chips) for c in range(2)]


def flip(count, mask):
    return [(i, i ^ mask) for i in range(count)]


def gather_tokens(rows):
    count = lax.axis_size("shard")
    pieces = [rows]
    for k in range(1, count // 2):
        pieces.append(lax.ppermute(rows, "shard", chip_shift(count, k)))
    near = jnp.concatenate(pieces, axis=0)
    far = lax.ppermute(near, "shard", flip(count, 1))
    return jnp.concatenate([near, far], axis=0)


def scatter_tokens(partial):
    count = lax.axis_size("shard")
    chips = count // 2
    half = partial.shape[0] // 2
    rows = half // chips
    got = lax.ppermute(partial[half:].astype(BF16), "shard", flip(count, 1))
    near = partial[:half] + got.astype(F32)
    total = near[:rows]
    for k in range(1, chips):
        piece = near[k * rows : (k + 1) * rows].astype(BF16)
        total = total + lax.ppermute(piece, "shard", chip_shift(count, -k)).astype(F32)
    return total


def replica_bits():
    return list(range(lax.axis_size("replica").bit_length() - 1))


def scatter_replicas(pieces, bits):
    count = lax.axis_size("replica")
    held = dict(enumerate(pieces))
    for b in bits:
        m = 1 << b
        keep = [p for p in held if not p & m]
        got = [lax.ppermute(held[p | m], "replica", flip(count, m)) for p in keep]
        held = {p: (held[p].astype(F32) + g.astype(F32)).astype(BF16) for p, g in zip(keep, got)}
    return held[0]


def gather_replicas(piece, bits):
    count = lax.axis_size("replica")
    held = {0: piece}
    for b in bits:
        m = 1 << b
        got = {p | m: lax.ppermute(a, "replica", flip(count, m)) for p, a in held.items()}
        held.update(got)
    return [held[p] for p in range(count)]


def swap_order(pieces):
    index = lax.axis_index("replica")
    stacked = jnp.stack(pieces) if isinstance(pieces, list) else pieces
    return [
        lax.dynamic_index_in_dim(stacked, index ^ p, 0, keepdims=False)
        for p in range(stacked.shape[0])
    ]


def exchange(blocks):
    return lax.all_to_all(blocks, "shard", 0, 0, tiled=True)


def attention_kernel(
    order_ref, q_ref, k_ref, v_ref, g_ref, cos_ref, lo_ref, hi_ref,
    mix_ref, gq_ref, gk_ref, gv_ref,
    q_sc, k_sc, v_sc, g_sc, dk_sc, dv_sc,
    *, blocks, block, step,
):
    tokens = blocks * block
    scale = HD**-0.5
    lanes = 2 * HD

    def turn(x, at, sign):
        cos, lo, hi = cos_ref[at, :], lo_ref[at, :], hi_ref[at, :]
        up = pltpu.roll(x, lanes - ROT // 2, 1)
        down = pltpu.roll(x, ROT // 2, 1)
        return x * cos + sign * (up * lo + down * hi)

    for b in range(blocks):
        src = pl.ds(pl.multiple_of(order_ref[b] * block, block), block)
        dst = pl.ds(b * block, block)
        q_sc[dst, :] = turn(q_ref[src, :], dst, 1.0).astype(BF16)
        k_sc[dst, :] = turn(k_ref[src, :], dst, 1.0).astype(BF16)
        v_sc[dst, :] = v_ref[src, :].astype(BF16)
        g_sc[dst, :] = g_ref[src, :]
    dk_sc[...] = jnp.zeros_like(dk_sc)
    dv_sc[...] = jnp.zeros_like(dv_sc)
    lane = lax.broadcasted_iota(jnp.int32, (1, lanes), 1)
    heads = [lane < HD, lane >= HD]
    for i in range(tokens // step):
        rows = pl.ds(i * step, step)
        width = (i + 1) * step
        q, g = q_sc[rows, :], g_sc[rows, :]
        k, v = k_sc[:width, :], v_sc[:width, :]
        seen = lax.broadcasted_iota(jnp.int32, (step, width), 1) <= i * step + (
            lax.broadcasted_iota(jnp.int32, (step, width), 0)
        )
        mixed = jnp.zeros((step, lanes), F32)
        dq = jnp.zeros((step, lanes), F32)
        for mine in heads:
            zero = jnp.zeros((), BF16)
            qh, gh = jnp.where(mine, q, zero), jnp.where(mine, g, zero)
            scores = dot(qh, k, (1, 1)) * scale
            scores = jnp.where(seen, scores, MASK_VALUE)
            top = jnp.max(scores, axis=1, keepdims=True)
            raised = jnp.exp(scores - top)
            probs = raised / jnp.sum(raised, axis=1, keepdims=True)
            weights = probs.astype(BF16)
            mixed = jnp.where(mine, dot(weights, v), mixed)
            grad_probs = dot(gh, v, (1, 1))
            delta = jnp.sum(probs * grad_probs, axis=1, keepdims=True)
            grad_scores = (probs * (grad_probs - delta)).astype(BF16)
            dq = jnp.where(mine, dot(grad_scores, k), dq)
            dk_sc[:width, :] += dot(grad_scores, qh, (0, 0))
            dv_sc[:width, :] += dot(weights, gh, (0, 0))
        dq = turn(dq * scale, rows, -1.0).astype(BF16)
        mixed = mixed.astype(BF16)
        for j in range(step // block):
            b = i * (step // block) + j
            out = pl.ds(pl.multiple_of(order_ref[b] * block, block), block)
            mix_ref[out, :] = mixed[j * block : (j + 1) * block]
            gq_ref[out, :] = dq[j * block : (j + 1) * block]
    for b in range(blocks):
        src = pl.ds(b * block, block)
        out = pl.ds(pl.multiple_of(order_ref[b] * block, block), block)
        gk_ref[out, :] = turn(dk_sc[src, :] * scale, src, -1.0).astype(BF16)
        gv_ref[out, :] = dv_sc[src, :].astype(BF16)


def attention(projected, grad_mixed, order, block):
    tokens, width = grad_mixed.shape
    lanes = 2 * HD
    pairs = width // lanes
    positions = jnp.arange(tokens, dtype=F32)
    frequencies = ROPE_BASE ** (-2.0 * jnp.arange(ROT // 2, dtype=F32) / ROT)
    angles = positions[:, None] * frequencies[None, :]
    cosine, sine = jnp.cos(angles), jnp.sin(angles)
    none, rest = jnp.zeros_like(sine), jnp.zeros((tokens, HD - ROT), F32)
    cos = jnp.concatenate([cosine, cosine, rest + 1.0] * 2, axis=1)
    low = jnp.concatenate([-sine, none, rest] * 2, axis=1)
    high = jnp.concatenate([none, sine, rest] * 2, axis=1)
    step = min(256, tokens)

    def column(offset):
        return pl.BlockSpec((tokens, lanes), lambda h, o: (0, offset + h))

    whole = pl.BlockSpec((tokens, lanes), lambda h, o: (0, 0))
    shape = jax.ShapeDtypeStruct((tokens, width), BF16)
    return pl.pallas_call(
        functools.partial(attention_kernel, blocks=tokens // block, block=block, step=step),
        out_shape=(shape,) * 4,
        grid_spec=pltpu.PrefetchScalarGridSpec(
            num_scalar_prefetch=1,
            grid=(pairs,),
            in_specs=[column(0), column(pairs), column(2 * pairs), column(0), whole, whole, whole],
            out_specs=[column(0)] * 4,
            scratch_shapes=[pltpu.VMEM((tokens, lanes), BF16)] * 4
            + [pltpu.VMEM((tokens, lanes), F32)] * 2,
        ),
        compiler_params=pltpu.CompilerParams(vmem_limit_bytes=48 * 2**20),
        cost_estimate=pl.CostEstimate(
            flops=14 * tokens * tokens * width,
            bytes_accessed=24 * tokens * width,
            transcendentals=tokens * tokens * (width // HD) // 2,
        ),
        name="attention",
    )(order, projected, projected, projected, grad_mixed, cos, low, high)


def normalize(values):
    center = values - jnp.mean(values, axis=-1, keepdims=True)
    spread = jnp.mean(center * center, axis=-1, keepdims=True)
    inverse = lax.rsqrt(spread + EPSILON)
    return center * inverse, inverse


def gelu_and_slope(u):
    inner = GELU_C * (u + 0.044715 * u * u * u)
    t = jnp.tanh(inner)
    slope = 0.5 * (1.0 + t) + 0.5 * u * (1.0 - t * t) * GELU_C * (1.0 + 3 * 0.044715 * u * u)
    return 0.5 * u * (1.0 + t), slope


def shards(
    block_in,
    norm_gain,
    norm_bias,
    attn_weight,
    attn_bias,
    dense_weight,
    dense_bias,
    up_weight,
    up_bias,
    down_weight,
    down_bias,
    cotangent,
):
    own, upstream = block_in[0], cotangent[0]
    tok_rows = own.shape[0]
    count, copies = lax.axis_size("shard"), lax.axis_size("replica")
    shard, replica = lax.axis_index("shard"), lax.axis_index("replica")
    chips = count // 2
    width = attn_weight.shape[0]
    ff = down_weight.shape[0]
    ff_part, row_part = ff // copies, width // copies
    bits = replica_bits()
    back = bits[::-1]

    up_part = lax.dynamic_index_in_dim(
        up_weight.reshape(width, count, copies, ff_part), replica, 2, keepdims=False
    )
    up_part = exchange(up_part.transpose(1, 0, 2)).reshape(D, ff_part)
    up_pieces = gather_replicas(up_part, bits)
    up_mine = jnp.concatenate(up_pieces, axis=1)
    attn_part = lax.dynamic_slice_in_dim(attn_weight, replica * row_part, row_part, 0)
    attn_part = attn_part.reshape(row_part, 3, count, width).transpose(2, 0, 1, 3)
    attn_part = exchange(attn_part.reshape(count, row_part, 3 * width))
    attn_mine = jnp.stack(swap_order(gather_replicas(attn_part, back)), axis=1)
    attn_mine = attn_mine.reshape(D, 3 * width)
    down_mine = jnp.concatenate(swap_order(down_weight.reshape(copies, ff_part, D)), axis=0)
    up_bias_mine = jnp.concatenate(swap_order(up_bias.reshape(copies, ff_part)))

    packed = jnp.concatenate(
        [
            norm_gain[:, None],
            norm_bias[:, None],
            attn_bias.reshape(width, 3),
            dense_bias[:, None],
            down_bias[:, None],
        ],
        axis=1,
    )
    small = lax.all_gather(packed, "shard", axis=0, tiled=True).astype(F32)
    gain, shift = small[:, 0], small[:, 1]
    attn_bias_full = small[:, 2:5].reshape(3, count, width)
    attn_bias_mine = lax.dynamic_index_in_dim(attn_bias_full, shard, 1, keepdims=False)
    out_bias = small[:, 5] + small[:, 6]

    tokens = gather_tokens(own).astype(F32)
    grads = gather_tokens(upstream)
    normed = (normalize(tokens)[0] * gain + shift).astype(BF16)

    hidden_pre = dot(normed, up_mine) + up_bias_mine.astype(F32)
    hidden, slope = gelu_and_slope(hidden_pre)
    hidden = hidden.astype(BF16)
    grad_pre = (dot(grads, down_mine, (1, 1)) * slope).astype(BF16)
    grad_down = [
        dot(hidden[:, p * ff_part : (p + 1) * ff_part], grads, (0, 0)).astype(BF16)
        for p in range(copies)
    ]
    grad_up = [
        dot(normed, grad_pre[:, p * ff_part : (p + 1) * ff_part], (0, 0)).astype(BF16)
        for p in range(copies)
    ]
    grad_down = gather_replicas(scatter_replicas(grad_down, bits), back)
    grad_up = scatter_replicas(grad_up, back)
    grad_up = exchange(grad_up.reshape(count, width, ff_part))
    grad_up = gather_replicas(grad_up, bits)

    projected = dot(normed, attn_mine) + attn_bias_mine.reshape(-1)
    grad_mixed = dot(grads, dense_weight, (1, 1)).astype(BF16)
    z, c = shard // 2, shard % 2
    place = jnp.arange(count, dtype=jnp.int32)
    order = ((place % 2) ^ c) * chips + (z - place // 2) % chips
    mixed, grad_q, grad_k, grad_v = attention(projected, grad_mixed, order, tok_rows)
    grad_projected = jnp.concatenate([grad_q, grad_k, grad_v], axis=1)
    grad_dense = dot(mixed, grads, (0, 0)).astype(BF16).reshape(copies, row_part, D)
    grad_dense = gather_replicas(scatter_replicas(swap_order(grad_dense), bits), back)
    grad_attn = dot(normed, grad_projected, (0, 0)).astype(BF16)
    grad_attn = grad_attn.reshape(count, copies, row_part, 3 * width).transpose(1, 0, 2, 3)
    grad_attn = swap_order(grad_attn)
    half = 3 * width // 2
    attn_halves = []
    for h, (first, second) in enumerate(((bits, back), (back, bits))):
        piece = scatter_replicas([a[..., h * half : (h + 1) * half] for a in grad_attn], first)
        attn_halves.append(gather_replicas(exchange(piece), second))

    branches = scatter_tokens(dot(hidden, down_mine) + dot(mixed, dense_weight))
    inputs = own.astype(F32)
    block_out = (inputs + branches + out_bias).astype(BF16)[None]
    part_rows = scatter_tokens(dot(grad_projected, attn_mine, (1, 1)) + dot(grad_pre, up_mine, (1, 1)))
    xhat, inverse = normalize(inputs)
    scaled = part_rows * gain
    grad_inputs = inverse * (
        scaled
        - jnp.mean(scaled, axis=-1, keepdims=True)
        - xhat * jnp.mean(scaled * xhat, axis=-1, keepdims=True)
    )
    grad_in = (upstream.astype(F32) + grad_inputs).astype(BF16)[None]

    sum_attn = jnp.sum(grad_projected.astype(F32), axis=0).reshape(3, 1, width)
    sum_up = jnp.sum(grad_pre.astype(F32), axis=0).reshape(copies, ff_part)
    sum_up = jnp.concatenate(swap_order(sum_up))
    sums = jnp.concatenate(
        [
            jnp.sum(part_rows * xhat, axis=0),
            jnp.sum(part_rows, axis=0),
            jnp.sum(upstream.astype(F32), axis=0),
            lax.dynamic_update_slice(jnp.zeros((3, count, width), F32), sum_attn, (0, shard, 0)).reshape(-1),
            lax.dynamic_update_slice(jnp.zeros((FF,), F32), sum_up, (shard * ff,)),
        ]
    )
    sums = lax.psum(sums, ("shard", "replica"))

    def mine(start, size):
        return lax.dynamic_slice(sums, (start + shard * size,), (size,))

    grad_out_bias = mine(2 * D, width)

    attn_whole = [jnp.stack(swap_order(a)) for a in attn_halves]
    attn_whole = jnp.concatenate(attn_whole, axis=-1)
    attn_whole = attn_whole.reshape(copies, count, row_part, 3, width).transpose(0, 2, 3, 1, 4)
    up_whole = jnp.stack(swap_order(grad_up)).transpose(2, 1, 0, 3)
    return (
        block_out,
        grad_in,
        mine(0, width),
        mine(D, width),
        attn_whole.reshape(width, 3 * D).astype(F32),
        mine(3 * D, 3 * width),
        jnp.concatenate(swap_order(grad_dense), axis=0).astype(F32),
        grad_out_bias,
        up_whole.reshape(width, FF).astype(F32),
        mine(6 * D, ff),
        jnp.concatenate(swap_order(grad_down), axis=0).astype(F32),
        grad_out_bias,
    )


def solution(mesh):
    vector, matrix = P("shard"), P("shard", None)
    rows = P("replica", "shard", None)
    return jax.shard_map(
        shards,
        mesh=mesh,
        in_specs=(rows, vector, vector, matrix, vector, matrix, vector, matrix, vector, matrix, vector, rows),
        out_specs=(rows, rows, vector, vector, matrix, vector, matrix, vector, matrix, vector, matrix, vector),
        check_vma=False,
    )
```

time: 2600 us -> 823 us (0.32)
  waiting for transfers between devices: 1980 us -> 312 us
  local copies, waits for them, and re-layouts: 378 us -> 119 us
  starting transfers between devices: 0.36 us -> 108 us
  matrix products: 178 us -> 86.5 us
  blocking collectives: 15.6 us -> 91.5 us
  other arithmetic: 23.3 us -> 63 us
    unnamed x11 -> x1, waiting for transfers between devices: 960 us -> 0.02 us
    all_gather x6 -> x0, waiting for transfers between devices: 799 us -> none  [the longest x1 232 us: shards(): lax.all_gather(up_weight, 'shard', axis=0, tiled=True)]
    ppermute x0 -> x52, waiting for transfers between devices: none -> 215 us  [the longest x21 112 us: gather_replicas(): lax.ppermute(a, 'replica', flip(count, m))]
    concatenate x2 -> x8, local copies, waits for them, and re-layouts: 162 us -> 12 us  [the longest x2 6.36 us: gather_tokens(): return jnp.concatenate([near, far], axis=0)]
    reshape x12 -> x7, local copies, waits for them, and re-layouts: 135 us -> 2.73 us  [the longest x1 1.7 us: shards(): attn_part = exchange(attn_part.reshape(count, row_part, 3 * width))]
    psum x1, waiting for transfers between devices: 216 us -> 85.6 us  [shards(): sums = lax.psum(sums, ('shard', 'replica'))]
    dot_general x19 -> x18, matrix products: 178 us -> 86.5 us  [dot(): lax.dot_general(left, right, (((contract[0],), (contract[1],)), ((), ()))...]
    ppermute x0 -> x52, starting transfers between devices: none -> 84 us  [the longest x6 35.8 us: scatter_tokens(): lax.ppermute(piece, 'shard', chip_shift(count, -k)).astype(F32)]
  transfers between devices with their start and end apart: 9 -> 58, of which waited for: 8 -> 25; matrix products, arithmetic and copies ran while one was open for 12% -> 29% of each run, Pallas kernels for 0% -> 3%
where the time goes in v1:
time: 823 us; the launch traced here: 815 us
  waiting for transfers between devices  312 us (38%)
  local copies, waits for them, and re-layouts  119 us (14%)
  starting transfers between devices  108 us (13%)
  blocking collectives  91.5 us (11%)
  matrix products  86.5 us (11%)
  other arithmetic  63 us (8%)
  Pallas kernels  20.6 us (3%)
  between operations  15.2 us (2%)
    ppermute x21, waiting for transfers between devices, gather_replicas(): lax.ppermute(a, 'replica', flip(count, m))  112 us
    all_gather x1, blocking collectives, shards(): small = lax.all_gather(packed, 'shard', axis=0, tiled=True).astype(F32)  91.5 us
    dot_general x18, matrix products, dot(): lax.dot_general(left, right, (((contract[0],), (contract[1],)), ((), ()))...  86.5 us
    psum x1, waiting for transfers between devices, shards(): sums = lax.psum(sums, ('shard', 'replica'))  85.6 us
    ppermute x6, waiting for transfers between devices, scatter_tokens(): lax.ppermute(piece, 'shard', chip_shift(count, -k)).astype(F32)  61.4 us
    ppermute x15, waiting for transfers between devices, scatter_replicas(): got = [lax.ppermute(held[p | m], 'replica', flip(count, m)) for p in keep]  40.9 us
    ppermute x6, starting transfers between devices, scatter_tokens(): lax.ppermute(piece, 'shard', chip_shift(count, -k)).astype(F32)  35.8 us
    unnamed x98, local copies, waits for them, and re-layouts  30.2 us
  transfers between devices with their start and end apart: 58, of which 25 were waited for; matrix products, arithmetic and copies ran while one was open for 29% of the time, Pallas kernels for 3%

profile of v1, /device:TPU:0, one launch (start us, length us, event | category | flops | bytes accessed | tf_op | source)
XLA Modules:
  0.0 815.4 jit_solution(6063242613161636770)
XLA Ops:
  17.6 4.7 all-to-all-start.1
  23.7 91.5 %all_gather.3 = bf16[2048,7]{0,1:T(8,128)(2,1)S(1)} all-gather(bf16[256,7]{0,1:T(8,128)(2,1)S(1)} %concatenate.67), channel_id=1, replica_groups=mesh['shard'=8,'replica'=4] {'shard'}, dimensions={0}, use_global_device_ids=true | all-gather | bytes 32256 | tf_op jit(solution)/shard_map/all_gather | solution.py:271
  115.5 6.4 copy.42
  122.5 4.4 dynamic-slice_bitcast_fusion.7
  139.8 4.4 all-to-all-start
  167.7 3.2 all-to-all-done
  172.4 4.6 collective-permute-done.8
  180.0 3.2 constant_dynamic-update-slice_fusion
  186.1 3.2 constant_dynamic-update-slice_fusion.5
  189.3 3.5 convolution_convert_fusion.10.g_ref
  192.7 3.4 fusion.2
  196.2 3.3 fusion.5
  199.5 9.9 %collective-permute-done.4 = bf16[2048,256]{1,0:T(8,128)(2,1)} collective-permute-done((bf16[2048,256]{1,0:T(8,128)(2,1)}, bf16[2048,256]{1,0:T(8,128)(2,1)}, u32[]{:S(2)}, u32[]{:S(2)}) %collective-permute-start.4) | collective-permute-done | bytes 1048608 | tf_op jit(solution)/shard_map/ppermute | solution.py:83
  210.0 15.0 %collective-permute-done.9 = bf16[8,64,768]{2,1,0:T(8,128)(2,1)S(1)} collective-permute-done((bf16[8,64,768]{2,1,0:T(8,128)(2,1)}, bf16[8,64,768]{2,1,0:T(8,128)(2,1)S(1)}, u32[]{:S(2)}, u32[]{:S(2)}) %collective-permute-start.9) | collective-permute-done | bytes 786464 | tf_op jit(solution)/shard_map/ppermute | solution.py:83
  227.6 5.1 convolution_add_fusion.2.q_ref.k_ref.v_ref
  232.7 20.6 %attention.1 = (bf16[1024,256]{1,0:T(8,128)(2,1)S(1)}, bf16[1024,256]{1,0:T(8,128)(2,1)S(1)}, bf16[1024,256]{1,0:T(8,128)(2,1)S(1)}, bf16[1024,256]{1,0:T(8,128)(2,1)S(1)}) custom-call(s32[8]{0:T(128)S(1)} %fusion.70.order_ref, f32[1024,768]{1,0:T(8,128)} %convolution_add_fusion.2.q_ref.k_ref.v_ref, f32[1024,768]{1,0:T(8,128)} %convolution_add_fusion.2.q_ref.k_ref.v_ref, ...), custom_call_target="tpu_custom_call" | custom-call | flops 3758096384 | bytes 6291456 | tf_op jit(solution)/shard_map/attention/pallas_call | solution.py:187
  253.4 5.7 fusion.87
  259.1 4.2 convolution_convert_fusion
  264.8 3.5 convolution_convert_fusion.9
  280.1 6.9 collective-permute-done.23
  291.2 7.8 collective-permute-done.34
  304.3 6.8 collective-permute-done.28
  311.6 7.8 collective-permute-done.24
  322.1 5.5 all-to-all-start.3
  328.2 9.1 %multiply_convert_fusion = (bf16[1024,1024]{1,0:T(8,128)(2,1)S(1)}, f32[1024,1024]{1,0:T(8,128)S(1)}) fusion(f32[1024]{0:T(1024)S(1)} %maximum_convert_fusion.3, bf16[1024,2048]{1,0:T(8,128)(2,1)} %copy-done.6, bf16[2048,256]{1,0:T(8,128)(2,1)} %collective-permute-done.6, bf16[2048,256]{1,0:T(8,128)(2,1)} %collective-permute-done.5, ...), kind=kOutput, calls=%fused_computation.29 | convolution fusion | flops 4322230272 | bytes 14684160 | tf_op jit(solution)/shard_map/dot_general | solution.py:25
  337.3 12.0 %convert_reduce_fusion.1 = (f32[1024]{0:T(1024)S(1)}, bf16[1024,1024]{1,0:T(8,128)(2,1)S(1)}) fusion(f32[1024,1024]{1,0:T(8,128)S(1)} %get-tuple-element.93, f32[1024]{0:T(1024)S(1)} %maximum_convert_fusion.3, bf16[1024,2048]{1,0:T(8,128)(2,1)} %constant_dynamic-update-slice_fusion.5, bf16[256,2048]{1,0:T(8,128)(2,1)S(1)} %copy-done.16, ...), kind=kOutput, calls=%fused_computation.28 | convolution fusion | flops 4334812160 | bytes 14688256 | tf_op jit(solution)/shard_map/dot_general | solution.py:25
  354.0 4.5 fusion.48
  358.5 4.4 convolution_convert_fusion.1
  362.9 4.5 convolution_convert_fusion.3
  367.4 9.2 %convolution_add_fusion.1 = f32[1024,2048]{1,0:T(8,128)S(1)} fusion(f32[1024,2048]{1,0:T(8,128)} %fusion.87, bf16[1024,1024]{1,0:T(8,128)(2,1)S(1)} %get-tuple-element.95, bf16[2048,256]{1,0:T(8,128)(2,1)} %collective-permute-done.6, bf16[2048,256]{1,0:T(8,128)(2,1)} %collective-permute-done.5, bf16[2048,256]{1,0:T(8,128)(2,1)} %collective-permute-done.4, ...), kind=kOutput, calls=%fused_computation.30 | convolution fusion | flops 4313841664 | bytes 23068672 | tf_op jit(solution)/shard_map/dot_general | solution.py:25
  381.5 3.4 copy-done.2
  387.1 4.9 all-to-all-start.2
  396.0 8.5 %all-to-all-done.2 = bf16[8,64,384]{2,1,0:T(8,128)(2,1)S(1)} async-done(((bf16[8,64,384]{2,1,0:T(8,128)(2,1)}), bf16[8,64,384]{2,1,0:T(8,128)(2,1)S(1)}, u32[]{:S(2)}, u32[]{:S(2)}) %all-to-all-start.2) | async-done | bytes 393248 | tf_op jit(solution)/shard_map/all_to_all | solution.py:98
  404.6 8.1 collective-permute-done.31
  414.7 3.9 fusion.15
  422.0 7.7 collective-permute-done.26
  432.5 5.6 collective-permute-done.33
  442.7 13.1 %collective-permute-done.25 = bf16[8,64,384]{2,1,0:T(8,128)(2,1)S(1)} collective-permute-done((bf16[8,64,384]{2,1,0:T(8,128)(2,1)S(1)}, bf16[8,64,384]{2,1,0:T(8,128)(2,1)S(1)}, u32[]{:S(2)}, u32[]{:S(2)}) %collective-permute-start.25) | collective-permute-done | bytes 393248 | tf_op jit(solution)/shard_map/ppermute | solution.py:83
  455.8 5.6 collective-permute-done.27
  464.8 5.5 fusion.21
  472.9 4.5 fusion.80
  478.6 9.0 %collective-permute-done.40 = bf16[2048,256]{1,0:T(8,128)(2,1)S(1)} collective-permute-done((bf16[2048,256]{1,0:T(8,128)(2,1)S(1)}, bf16[2048,256]{1,0:T(8,128)(2,1)S(1)}, u32[]{:S(2)}, u32[]{:S(2)}) %collective-permute-start.40) | collective-permute-done | bytes 1048608 | tf_op jit(solution)/shard_map/ppermute | solution.py:73
  489.9 3.2 collective-permute-start.20
  495.6 4.2 all-to-all-start.4
  499.9 3.7 collective-permute-start.19
  503.7 3.7 fusion.81
  507.5 16.6 %collective-permute-start.17 = (bf16[128,2048]{1,0:T(8,128)(2,1)S(1)}, bf16[128,2048]{1,0:T(8,128)(2,1)S(1)}, u32[]{:S(2)}, u32[]{:S(2)}) collective-permute-start(bf16[128,2048]{1,0:T(8,128)(2,1)S(1)} %get-tuple-element.57), channel_id=1, source_target_pairs={{0,8},{4,12},{8,16},{12,20},{16,24},{20,28},{24,0},{28,4},{1,9},{5... | collective-permute-start | bytes 1572872 | tf_op jit(solution)/shard_map/ppermute | solution.py:59
  524.1 7.4 collective-permute-done.20
  532.6 14.2 %collective-permute-done.19 = bf16[128,2048]{1,0:T(8,128)(2,1)S(1)} collective-permute-done((bf16[128,2048]{1,0:T(8,128)(2,1)S(1)}, bf16[128,2048]{1,0:T(8,128)(2,1)S(1)}, u32[]{:S(2)}, u32[]{:S(2)}) %collective-permute-start.19) | collective-permute-done | bytes 524320 | tf_op jit(solution)/shard_map/ppermute | solution.py:59
  546.8 9.0 %collective-permute-start.15 = (bf16[128,2048]{1,0:T(8,128)(2,1)S(1)}, bf16[128,2048]{1,0:T(8,128)(2,1)S(1)}, u32[]{:S(2)}, u32[]{:S(2)}) collective-permute-start(bf16[128,2048]{1,0:T(8,128)(2,1)S(1)} %get-tuple-element.56), channel_id=1, source_target_pairs={{0,24},{4,28},{8,0},{12,4},{16,8},{20,12},{24,16},{28,20},{1,25},{... | collective-permute-start | bytes 1572872 | tf_op jit(solution)/shard_map/ppermute | solution.py:59
  558.8 28.7 %collective-permute-done.16 = bf16[128,2048]{1,0:T(8,128)(2,1)S(1)} collective-permute-done((bf16[128,2048]{1,0:T(8,128)(2,1)S(1)}, bf16[128,2048]{1,0:T(8,128)(2,1)S(1)}, u32[]{:S(2)}, u32[]{:S(2)}) %collective-permute-start.16) | collective-permute-done | bytes 524320 | tf_op jit(solution)/shard_map/ppermute | solution.py:59
  587.5 11.1 %collective-permute-done.15 = bf16[128,2048]{1,0:T(8,128)(2,1)S(1)} collective-permute-done((bf16[128,2048]{1,0:T(8,128)(2,1)S(1)}, bf16[128,2048]{1,0:T(8,128)(2,1)S(1)}, u32[]{:S(2)}, u32[]{:S(2)}) %collective-permute-start.15) | collective-permute-done | bytes 524320 | tf_op jit(solution)/shard_map/ppermute | solution.py:59
  598.7 3.5 convert_reduce_fusion.4
  608.9 4.2 maximum_convert_fusion.1
  613.0 10.7 %reshape.193 = f32[4,8,64,3,256]{4,3,2,1,0:T(4,128)} reshape(f32[4,8,64,768]{3,2,1,0:T(8,128)} %maximum_convert_fusion.1) | data formatting | bytes 12582912 | tf_op jit(solution)/shard_map/convert_element_type | solution.py:357
  623.7 9.7 %copy.47 = f32[4,64,3,8,256]{4,3,2,1,0:T(8,128)} copy(f32[4,64,3,8,256]{4,2,1,3,0:T(4,128)} %bitcast.146) | data formatting | bytes 12582912 | tf_op jit(solution)/shard_map/convert_element_type | solution.py:357
  633.5 7.3 reshape.189
  640.8 85.6 %all-reduce.2.cloned.1.call-done = f32[20480]{0:T(1024)} async-done(((f32[20480]{0:T(1024)}), f32[20480]{0:T(1024)}) %all-reduce.2.cloned.1.call-update) | async-done | bytes 81936 | tf_op jit(solution)/shard_map/psum | solution.py:341
  735.1 3.9 maximum_convert_fusion
  739.0 17.6 %collective-permute-done.44 = bf16[8,256,256]{2,1,0:T(8,128)(2,1)S(1)} collective-permute-done((bf16[8,256,256]{2,1,0:T(8,128)(2,1)}, bf16[8,256,256]{2,1,0:T(8,128)(2,1)S(1)}, u32[]{:S(2)}, u32[]{:S(2)}) %collective-permute-start.44) | collective-permute-done | bytes 1048608 | tf_op jit(solution)/shard_map/ppermute | solution.py:83
  756.5 22.1 %collective-permute-done.45 = bf16[8,256,256]{2,1,0:T(8,128)(2,1)S(1)} collective-permute-done((bf16[8,256,256]{2,1,0:T(8,128)(2,1)}, bf16[8,256,256]{2,1,0:T(8,128)(2,1)S(1)}, u32[]{:S(2)}, u32[]{:S(2)}) %collective-permute-start.45) | collective-permute-done | bytes 1048608 | tf_op jit(solution)/shard_map/ppermute | solution.py:83
  780.9 3.9 convert_bitcast_fusion
  784.9 12.1 %copy.48 = f32[256,8,4,256]{3,2,1,0:T(4,128)} copy(f32[256,8,4,256]{3,0,1,2:T(8,128)} %convert_bitcast_fusion) | data formatting | bytes 16777216 | tf_op jit(solution)/shard_map/convert_element_type | solution.py:361
  797.0 10.9 %reshape.192 = f32[256,8192]{1,0:T(8,128)} reshape(f32[256,8,4,256]{3,2,1,0:T(4,128)} %copy.48) | data formatting | bytes 16777216 | tf_op jit(solution)/shard_map/convert_element_type | solution.py:361
  (271 shorter events, 148.8 us)
Async XLA Ops:
  7.2 126.9 %collective-permute-start = (bf16[128,2048]{1,0:T(8,128)(2,1)}, bf16[128,2048]{1,0:T(8,128)(2,1)}, u32[]{:S(2)}, u32[]{:S(2)}) collective-permute-start(bf16[128,2048]{1,0:T(8,128)(2,1)} %bitcast.147), channel_id=1, source_target_pairs={{0,8},{4,12},{8,16},{12,20},{16,24},{20,28},{24,0},{28,4},{1,9},{5... | collective-permute-start | bytes 1572872 | tf_op jit(solution)/shard_map/ppermute | solution.py:43
  10.3 126.1 %collective-permute-start.1 = (bf16[128,2048]{1,0:T(8,128)(2,1)}, bf16[128,2048]{1,0:T(8,128)(2,1)}, u32[]{:S(2)}, u32[]{:S(2)}) collective-permute-start(bf16[128,2048]{1,0:T(8,128)(2,1)} %bitcast.148), channel_id=1, source_target_pairs={{0,16},{4,20},{8,24},{12,28},{16,0},{20,4},{24,8},{28,12},{1,17},{... | collective-permute-start | bytes 1572872 | tf_op jit(solution)/shard_map/ppermute | solution.py:43
  12.9 123.5 %collective-permute-start.2 = (bf16[128,2048]{1,0:T(8,128)(2,1)}, bf16[128,2048]{1,0:T(8,128)(2,1)}, u32[]{:S(2)}, u32[]{:S(2)}) collective-permute-start(bf16[128,2048]{1,0:T(8,128)(2,1)} %bitcast.149), channel_id=1, source_target_pairs={{0,24},{4,28},{8,0},{12,4},{16,8},{20,12},{24,16},{28,20},{1,25},{... | collective-permute-start | bytes 1572872 | tf_op jit(solution)/shard_map/ppermute | solution.py:43
  14.2 135.6 %collective-permute-start.10 = (bf16[128,2048]{1,0:T(8,128)(2,1)}, bf16[128,2048]{1,0:T(8,128)(2,1)}, u32[]{:S(2)}, u32[]{:S(2)}) collective-permute-start(bf16[128,2048]{1,0:T(8,128)(2,1)} %bitcast.23), channel_id=1, source_target_pairs={{0,8},{4,12},{8,16},{12,20},{16,24},{20,28},{24,0},{28,4},{1,9},{5... | collective-permute-start | bytes 1572872 | tf_op jit(solution)/shard_map/ppermute | solution.py:43
  14.9 134.9 %collective-permute-start.11 = (bf16[128,2048]{1,0:T(8,128)(2,1)}, bf16[128,2048]{1,0:T(8,128)(2,1)}, u32[]{:S(2)}, u32[]{:S(2)}) collective-permute-start(bf16[128,2048]{1,0:T(8,128)(2,1)} %bitcast.23), channel_id=1, source_target_pairs={{0,16},{4,20},{8,24},{12,28},{16,0},{20,4},{24,8},{28,12},{1,17},{... | collective-permute-start | bytes 1572872 | tf_op jit(solution)/shard_map/ppermute | solution.py:43
  17.6 122.2 %all-to-all-start.1 = ((bf16[8,64,768]{2,1,0:T(8,128)(2,1)}), bf16[8,64,768]{2,1,0:T(8,128)(2,1)}, u32[]{:S(2)}, u32[]{:S(2)}) async-start(bf16[8,64,768]{2,1,0:T(8,128)(2,1)} %reshape.180), calls=%async_computation.1 | async-start | bytes 1572864 | tf_op jit(solution)/shard_map/all_to_all | solution.py:98
  134.1 15.8 %collective-permute-start.12 = (bf16[128,2048]{1,0:T(8,128)(2,1)}, bf16[128,2048]{1,0:T(8,128)(2,1)}, u32[]{:S(2)}, u32[]{:S(2)}) collective-permute-start(bf16[128,2048]{1,0:T(8,128)(2,1)} %bitcast.23), channel_id=1, source_target_pairs={{0,24},{4,28},{8,0},{12,4},{16,8},{20,12},{24,16},{28,20},{1,25},{... | collective-permute-start | bytes 1572872 | tf_op jit(solution)/shard_map/ppermute | solution.py:43
  139.3 39.2 %collective-permute-start.3 = (bf16[512,2048]{1,0:T(8,128)(2,1)}, bf16[512,2048]{1,0:T(8,128)(2,1)}, u32[]{:S(2)}, u32[]{:S(2)}) collective-permute-start(bf16[512,2048]{1,0:T(8,128)(2,1)} %pad_maximum_fusion.6), channel_id=1, source_target_pairs={{0,4},{4,0},{8,12},{12,8},{16,20},{20,16},{24,28},{28,24},{1,5},{5... | collective-permute-start | bytes 6291464 | tf_op jit(solution)/shard_map/ppermute | solution.py:45
  139.8 31.1 %all-to-all-start = ((bf16[8,256,256]{2,1,0:T(8,128)(2,1)}), bf16[8,256,256]{2,1,0:T(8,128)(2,1)}, u32[]{:S(2)}, u32[]{:S(2)}) async-start(bf16[8,256,256]{2,1,0:T(8,128)(2,1)} %copy.44), calls=%async_computation | async-start | bytes 2097152 | tf_op jit(solution)/shard_map/all_to_all | solution.py:98
  152.9 33.1 %collective-permute-start.13 = (bf16[512,2048]{1,0:T(8,128)(2,1)}, bf16[512,2048]{1,0:T(8,128)(2,1)}, u32[]{:S(2)}, u32[]{:S(2)}) collective-permute-start(bf16[512,2048]{1,0:T(8,128)(2,1)} %pad_maximum_fusion.7), channel_id=1, source_target_pairs={{0,4},{4,0},{8,12},{12,8},{16,20},{20,16},{24,28},{28,24},{1,5},{5... | collective-permute-start | bytes 6291464 | tf_op jit(solution)/shard_map/ppermute | solution.py:45
  157.1 19.8 %collective-permute-start.8 = (bf16[8,64,768]{2,1,0:T(8,128)(2,1)}, bf16[8,64,768]{2,1,0:T(8,128)(2,1)}, u32[]{:S(2)}, u32[]{:S(2)}) collective-permute-start(bf16[8,64,768]{2,1,0:T(8,128)(2,1)} %all-to-all-done.1), channel_id=1, source_target_pairs={{0,2},{1,3},{2,0},{3,1},{4,6},{5,7},{6,4},{7,5},{8,10},{9,11},{10,... | collective-permute-start | bytes 2359304 | tf_op jit(solution)/shard_map/ppermute | solution.py:83
  166.2 43.7 %collective-permute-start.7 = (bf16[8,64,768]{2,1,0:T(8,128)(2,1)}, bf16[8,64,768]{2,1,0:T(8,128)(2,1)}, u32[]{:S(2)}, u32[]{:S(2)}) collective-permute-start(bf16[8,64,768]{2,1,0:T(8,128)(2,1)} %all-to-all-done.1), channel_id=1, source_target_pairs={{0,1},{1,0},{2,3},{3,2},{4,5},{5,4},{6,7},{7,6},{8,9},{9,8},{10,11... | collective-permute-start | bytes 2359304 | tf_op jit(solution)/shard_map/ppermute | solution.py:83
  170.9 38.6 %collective-permute-start.4 = (bf16[2048,256]{1,0:T(8,128)(2,1)}, bf16[2048,256]{1,0:T(8,128)(2,1)}, u32[]{:S(2)}, u32[]{:S(2)}) collective-permute-start(bf16[2048,256]{1,0:T(8,128)(2,1)} %bitcast.7), channel_id=1, source_target_pairs={{0,1},{1,0},{2,3},{3,2},{4,5},{5,4},{6,7},{7,6},{8,9},{9,8},{10,11... | collective-permute-start | bytes 3145736 | tf_op jit(solution)/shard_map/ppermute | solution.py:83
  177.0 151.2 %collective-permute-start.5 = (bf16[2048,256]{1,0:T(8,128)(2,1)}, bf16[2048,256]{1,0:T(8,128)(2,1)}, u32[]{:S(2)}, u32[]{:S(2)}) collective-permute-start(bf16[2048,256]{1,0:T(8,128)(2,1)} %bitcast.7), channel_id=1, source_target_pairs={{0,2},{1,3},{2,0},{3,1},{4,6},{5,7},{6,4},{7,5},{8,10},{9,11},{10,... | collective-permute-start | bytes 3145736 | tf_op jit(solution)/shard_map/ppermute | solution.py:83
  178.5 46.5 %collective-permute-start.9 = (bf16[8,64,768]{2,1,0:T(8,128)(2,1)}, bf16[8,64,768]{2,1,0:T(8,128)(2,1)S(1)}, u32[]{:S(2)}, u32[]{:S(2)}) collective-permute-start(bf16[8,64,768]{2,1,0:T(8,128)(2,1)} %collective-permute-done.8), channel_id=1, source_target_pairs={{0,1},{1,0},{2,3},{3,2},{4,5},{5,4},{6,7},{7,6},{8,9},{9,8},{10,11... | collective-permute-start | bytes 2359304 | tf_op jit(solution)/shard_map/ppermute | solution.py:83
  199.5 59.6 %copy-start.6 = (bf16[1024,2048]{1,0:T(8,128)(2,1)}, bf16[1024,2048]{1,0:T(8,128)(2,1)S(1)}, u32[]{:S(2)}) copy-start(bf16[1024,2048]{1,0:T(8,128)(2,1)S(1)} %fusion.5) | copy-start | bytes 12582916
  209.5 118.7 %collective-permute-start.6 = (bf16[2048,256]{1,0:T(8,128)(2,1)}, bf16[2048,256]{1,0:T(8,128)(2,1)}, u32[]{:S(2)}, u32[]{:S(2)}) collective-permute-start(bf16[2048,256]{1,0:T(8,128)(2,1)} %collective-permute-done.4), channel_id=1, source_target_pairs={{0,2},{1,3},{2,0},{3,1},{4,6},{5,7},{6,4},{7,5},{8,10},{9,11},{10,... | collective-permute-start | bytes 3145736 | tf_op jit(solution)/shard_map/ppermute | solution.py:83
  269.3 9.3 %collective-permute-start.35 = (bf16[64,2048]{1,0:T(8,128)(2,1)S(1)}, bf16[64,2048]{1,0:T(8,128)(2,1)S(1)}, u32[]{:S(2)}, u32[]{:S(2)}) collective-permute-start(bf16[64,2048]{1,0:T(8,128)(2,1)S(1)} %get-tuple-element.72), channel_id=1, source_target_pairs={{0,1},{1,0},{2,3},{3,2},{4,5},{5,4},{6,7},{7,6},{8,9},{9,8},{10,11... | collective-permute-start | bytes 786440 | tf_op jit(solution)/shard_map/ppermute | solution.py:73
  271.9 15.1 %collective-permute-start.23 = (bf16[8,64,384]{2,1,0:T(8,128)(2,1)S(1)}, bf16[8,64,384]{2,1,0:T(8,128)(2,1)S(1)}, u32[]{:S(2)}, u32[]{:S(2)}) collective-permute-start(bf16[8,64,384]{2,1,0:T(8,128)(2,1)S(1)} %get-tuple-element.75), channel_id=1, source_target_pairs={{0,1},{1,0},{2,3},{3,2},{4,5},{5,4},{6,7},{7,6},{8,9},{9,8},{10,11... | collective-permute-start | bytes 1179656 | tf_op jit(solution)/shard_map/ppermute | solution.py:73
  273.6 26.0 %collective-permute-start.22 = (bf16[8,64,384]{2,1,0:T(8,128)(2,1)S(1)}, bf16[8,64,384]{2,1,0:T(8,128)(2,1)S(1)}, u32[]{:S(2)}, u32[]{:S(2)}) collective-permute-start(bf16[8,64,384]{2,1,0:T(8,128)(2,1)S(1)} %slice.158), channel_id=1, source_target_pairs={{0,1},{1,0},{2,3},{3,2},{4,5},{5,4},{6,7},{7,6},{8,9},{9,8},{10,11... | collective-permute-start | bytes 1179656 | tf_op jit(solution)/shard_map/ppermute | solution.py:73
  278.6 9.9 %collective-permute-start.29 = (bf16[8,64,384]{2,1,0:T(8,128)(2,1)S(1)}, bf16[8,64,384]{2,1,0:T(8,128)(2,1)S(1)}, u32[]{:S(2)}, u32[]{:S(2)}) collective-permute-start(bf16[8,64,384]{2,1,0:T(8,128)(2,1)S(1)} %get-tuple-element.76), channel_id=1, source_target_pairs={{0,2},{1,3},{2,0},{3,1},{4,6},{5,7},{6,4},{7,5},{8,10},{9,11},{10,... | collective-permute-start | bytes 1179656 | tf_op jit(solution)/shard_map/ppermute | solution.py:73
  287.0 12.0 %collective-permute-start.34 = (bf16[64,2048]{1,0:T(8,128)(2,1)S(1)}, bf16[64,2048]{1,0:T(8,128)(2,1)S(1)}, u32[]{:S(2)}, u32[]{:S(2)}) collective-permute-start(bf16[64,2048]{1,0:T(8,128)(2,1)S(1)} %get-tuple-element.71), channel_id=1, source_target_pairs={{0,1},{1,0},{2,3},{3,2},{4,5},{5,4},{6,7},{7,6},{8,9},{9,8},{10,11... | collective-permute-start | bytes 786440 | tf_op jit(solution)/shard_map/ppermute | solution.py:73
  288.5 12.6 %collective-permute-start.36 = (bf16[64,2048]{1,0:T(8,128)(2,1)S(1)}, bf16[64,2048]{1,0:T(8,128)(2,1)S(1)}, u32[]{:S(2)}, u32[]{:S(2)}) collective-permute-start(bf16[64,2048]{1,0:T(8,128)(2,1)S(1)} %fusion.60), channel_id=1, source_target_pairs={{0,2},{1,3},{2,0},{3,1},{4,6},{5,7},{6,4},{7,5},{8,10},{9,11},{10,... | collective-permute-start | bytes 786440 | tf_op jit(solution)/shard_map/ppermute | solution.py:73
  299.0 12.1 %collective-permute-start.28 = (bf16[8,64,384]{2,1,0:T(8,128)(2,1)S(1)}, bf16[8,64,384]{2,1,0:T(8,128)(2,1)S(1)}, u32[]{:S(2)}, u32[]{:S(2)}) collective-permute-start(bf16[8,64,384]{2,1,0:T(8,128)(2,1)S(1)} %slice.162), channel_id=1, source_target_pairs={{0,2},{1,3},{2,0},{3,1},{4,6},{5,7},{6,4},{7,5},{8,10},{9,11},{10,... | collective-permute-start | bytes 1179656 | tf_op jit(solution)/shard_map/ppermute | solution.py:73
  299.5 19.8 %collective-permute-start.24 = (bf16[8,64,384]{2,1,0:T(8,128)(2,1)S(1)}, bf16[8,64,384]{2,1,0:T(8,128)(2,1)S(1)}, u32[]{:S(2)}, u32[]{:S(2)}) collective-permute-start(bf16[8,64,384]{2,1,0:T(8,128)(2,1)S(1)} %add_convert_fusion.4), channel_id=1, source_target_pairs={{0,2},{1,3},{2,0},{3,1},{4,6},{5,7},{6,4},{7,5},{8,10},{9,11},{10,... | collective-permute-start | bytes 1179656 | tf_op jit(solution)/shard_map/ppermute | solution.py:73
  301.0 19.8 %collective-permute-start.30 = (bf16[8,64,384]{2,1,0:T(8,128)(2,1)S(1)}, bf16[8,64,384]{2,1,0:T(8,128)(2,1)S(1)}, u32[]{:S(2)}, u32[]{:S(2)}) collective-permute-start(bf16[8,64,384]{2,1,0:T(8,128)(2,1)S(1)} %add_convert_fusion.1), channel_id=1, source_target_pairs={{0,1},{1,0},{2,3},{3,2},{4,5},{5,4},{6,7},{7,6},{8,9},{9,8},{10,11... | collective-permute-start | bytes 1179656 | tf_op jit(solution)/shard_map/ppermute | solution.py:73
  311.1 16.5 %collective-permute-start.38 = (bf16[64,2048]{1,0:T(8,128)(2,1)}, bf16[64,2048]{1,0:T(8,128)(2,1)}, u32[]{:S(2)}, u32[]{:S(2)}) collective-permute-start(bf16[64,2048]{1,0:T(8,128)(2,1)} %add_convert_fusion.6), channel_id=1, source_target_pairs={{0,2},{1,3},{2,0},{3,1},{4,6},{5,7},{6,4},{7,5},{8,10},{9,11},{10,... | collective-permute-start | bytes 786440 | tf_op jit(solution)/shard_map/ppermute | solution.py:83
  319.4 72.7 %collective-permute-start.37 = (bf16[64,2048]{1,0:T(8,128)(2,1)}, bf16[64,2048]{1,0:T(8,128)(2,1)}, u32[]{:S(2)}, u32[]{:S(2)}) collective-permute-start(bf16[64,2048]{1,0:T(8,128)(2,1)} %add_convert_fusion.6), channel_id=1, source_target_pairs={{0,1},{1,0},{2,3},{3,2},{4,5},{5,4},{6,7},{7,6},{8,9},{9,8},{10,11... | collective-permute-start | bytes 786440 | tf_op jit(solution)/shard_map/ppermute | solution.py:83
  322.1 65.1 %all-to-all-start.3 = ((bf16[8,64,384]{2,1,0:T(8,128)(2,1)}), bf16[8,64,384]{2,1,0:T(8,128)(2,1)S(1)}, u32[]{:S(2)}, u32[]{:S(2)}) async-start(bf16[8,64,384]{2,1,0:T(8,128)(2,1)} %get-tuple-element.74), calls=%async_computation.3 | async-start | bytes 786432 | tf_op jit(solution)/shard_map/all_to_all | solution.py:98
  327.6 65.4 %collective-permute-start.39 = (bf16[64,2048]{1,0:T(8,128)(2,1)}, bf16[64,2048]{1,0:T(8,128)(2,1)}, u32[]{:S(2)}, u32[]{:S(2)}) collective-permute-start(bf16[64,2048]{1,0:T(8,128)(2,1)} %collective-permute-done.38), channel_id=1, source_target_pairs={{0,1},{1,0},{2,3},{3,2},{4,5},{5,4},{6,7},{7,6},{8,9},{9,8},{10,11... | collective-permute-start | bytes 786440 | tf_op jit(solution)/shard_map/ppermute | solution.py:83
  378.4 93.4 %collective-permute-start.18 = (bf16[512,2048]{1,0:T(8,128)(2,1)}, bf16[512,2048]{1,0:T(8,128)(2,1)}, u32[]{:S(2)}, u32[]{:S(2)}) collective-permute-start(bf16[512,2048]{1,0:T(8,128)(2,1)} %slice.213), channel_id=1, source_target_pairs={{0,4},{4,0},{8,12},{12,8},{16,20},{20,16},{24,28},{28,24},{1,5},{5... | collective-permute-start | bytes 6291464 | tf_op jit(solution)/shard_map/ppermute | solution.py:54
  378.5 34.7 %collective-permute-start.47 = (bf16[256,2048]{1,0:T(8,128)(2,1)}, bf16[256,2048]{1,0:T(8,128)(2,1)}, u32[]{:S(2)}, u32[]{:S(2)}) collective-permute-start(bf16[256,2048]{1,0:T(8,128)(2,1)} %convolution_convert_fusion.1), channel_id=1, source_target_pairs={{0,1},{1,0},{2,3},{3,2},{4,5},{5,4},{6,7},{7,6},{8,9},{9,8},{10,11... | collective-permute-start | bytes 3145736 | tf_op jit(solution)/shard_map/ppermute | solution.py:73
  386.6 45.2 %collective-permute-start.41 = (bf16[2048,256]{1,0:T(8,128)(2,1)}, bf16[2048,256]{1,0:T(8,128)(2,1)}, u32[]{:S(2)}, u32[]{:S(2)}) collective-permute-start(bf16[2048,256]{1,0:T(8,128)(2,1)} %convolution_convert_fusion.5), channel_id=1, source_target_pairs={{0,2},{1,3},{2,0},{3,1},{4,6},{5,7},{6,4},{7,5},{8,10},{9,11},{10,... | collective-permute-start | bytes 3145736 | tf_op jit(solution)/shard_map/ppermute | solution.py:73
  387.1 17.4 %all-to-all-start.2 = ((bf16[8,64,384]{2,1,0:T(8,128)(2,1)}), bf16[8,64,384]{2,1,0:T(8,128)(2,1)S(1)}, u32[]{:S(2)}, u32[]{:S(2)}) async-start(bf16[8,64,384]{2,1,0:T(8,128)(2,1)} %get-tuple-element.73), calls=%async_computation.2 | async-start | bytes 786432 | tf_op jit(solution)/shard_map/all_to_all | solution.py:98
  392.1 20.6 %collective-permute-start.31 = (bf16[8,64,384]{2,1,0:T(8,128)(2,1)S(1)}, bf16[8,64,384]{2,1,0:T(8,128)(2,1)S(1)}, u32[]{:S(2)}, u32[]{:S(2)}) collective-permute-start(bf16[8,64,384]{2,1,0:T(8,128)(2,1)S(1)} %all-to-all-done.3), channel_id=1, source_target_pairs={{0,1},{1,0},{2,3},{3,2},{4,5},{5,4},{6,7},{7,6},{8,9},{9,8},{10,11... | collective-permute-start | bytes 1179656 | tf_op jit(solution)/shard_map/ppermute | solution.py:83
  394.4 26.8 %collective-permute-start.32 = (bf16[8,64,384]{2,1,0:T(8,128)(2,1)S(1)}, bf16[8,64,384]{2,1,0:T(8,128)(2,1)S(1)}, u32[]{:S(2)}, u32[]{:S(2)}) collective-permute-start(bf16[8,64,384]{2,1,0:T(8,128)(2,1)S(1)} %all-to-all-done.3), channel_id=1, source_target_pairs={{0,2},{1,3},{2,0},{3,1},{4,6},{5,7},{6,4},{7,5},{8,10},{9,11},{10,... | collective-permute-start | bytes 1179656 | tf_op jit(solution)/shard_map/ppermute | solution.py:83
  412.7 17.1 %collective-permute-start.26 = (bf16[8,64,384]{2,1,0:T(8,128)(2,1)S(1)}, bf16[8,64,384]{2,1,0:T(8,128)(2,1)S(1)}, u32[]{:S(2)}, u32[]{:S(2)}) collective-permute-start(bf16[8,64,384]{2,1,0:T(8,128)(2,1)S(1)} %all-to-all-done.2), channel_id=1, source_target_pairs={{0,2},{1,3},{2,0},{3,1},{4,6},{5,7},{6,4},{7,5},{8,10},{9,11},{10,... | collective-permute-start | bytes 1179656 | tf_op jit(solution)/shard_map/ppermute | solution.py:83
  413.2 25.0 %collective-permute-start.33 = (bf16[8,64,384]{2,1,0:T(8,128)(2,1)S(1)}, bf16[8,64,384]{2,1,0:T(8,128)(2,1)S(1)}, u32[]{:S(2)}, u32[]{:S(2)}) collective-permute-start(bf16[8,64,384]{2,1,0:T(8,128)(2,1)S(1)} %collective-permute-done.31), channel_id=1, source_target_pairs={{0,2},{1,3},{2,0},{3,1},{4,6},{5,7},{6,4},{7,5},{8,10},{9,11},{10,... | collective-permute-start | bytes 1179656 | tf_op jit(solution)/shard_map/ppermute | solution.py:83
  421.3 42.5 %collective-permute-start.46 = (bf16[256,2048]{1,0:T(8,128)(2,1)S(1)}, bf16[256,2048]{1,0:T(8,128)(2,1)S(1)}, u32[]{:S(2)}, u32[]{:S(2)}) collective-permute-start(bf16[256,2048]{1,0:T(8,128)(2,1)S(1)} %copy-done.31), channel_id=1, source_target_pairs={{0,1},{1,0},{2,3},{3,2},{4,5},{5,4},{6,7},{7,6},{8,9},{9,8},{10,11... | collective-permute-start | bytes 3145736 | tf_op jit(solution)/shard_map/ppermute | solution.py:73
  429.7 35.1 %collective-permute-start.48 = (bf16[256,2048]{1,0:T(8,128)(2,1)S(1)}, bf16[256,2048]{1,0:T(8,128)(2,1)S(1)}, u32[]{:S(2)}, u32[]{:S(2)}) collective-permute-start(bf16[256,2048]{1,0:T(8,128)(2,1)S(1)} %fusion.15), channel_id=1, source_target_pairs={{0,2},{1,3},{2,0},{3,1},{4,6},{5,7},{6,4},{7,5},{8,10},{9,11},{10,... | collective-permute-start | bytes 3145736 | tf_op jit(solution)/shard_map/ppermute | solution.py:73
  431.8 24.0 %collective-permute-start.25 = (bf16[8,64,384]{2,1,0:T(8,128)(2,1)S(1)}, bf16[8,64,384]{2,1,0:T(8,128)(2,1)S(1)}, u32[]{:S(2)}, u32[]{:S(2)}) collective-permute-start(bf16[8,64,384]{2,1,0:T(8,128)(2,1)S(1)} %all-to-all-done.2), channel_id=1, source_target_pairs={{0,1},{1,0},{2,3},{3,2},{4,5},{5,4},{6,7},{7,6},{8,9},{9,8},{10,11... | collective-permute-start | bytes 1179656 | tf_op jit(solution)/shard_map/ppermute | solution.py:83
  438.1 23.3 %collective-permute-start.27 = (bf16[8,64,384]{2,1,0:T(8,128)(2,1)S(1)}, bf16[8,64,384]{2,1,0:T(8,128)(2,1)S(1)}, u32[]{:S(2)}, u32[]{:S(2)}) collective-permute-start(bf16[8,64,384]{2,1,0:T(8,128)(2,1)S(1)} %collective-permute-done.26), channel_id=1, source_target_pairs={{0,1},{1,0},{2,3},{3,2},{4,5},{5,4},{6,7},{7,6},{8,9},{9,8},{10,11... | collective-permute-start | bytes 1179656 | tf_op jit(solution)/shard_map/ppermute | solution.py:83
  455.8 44.1 %collective-permute-start.14 = (bf16[512,2048]{1,0:T(8,128)(2,1)}, bf16[512,2048]{1,0:T(8,128)(2,1)}, u32[]{:S(2)}, u32[]{:S(2)}) collective-permute-start(bf16[512,2048]{1,0:T(8,128)(2,1)} %slice.214), channel_id=1, source_target_pairs={{0,4},{4,0},{8,12},{12,8},{16,20},{20,16},{24,28},{28,24},{1,5},{5... | collective-permute-start | bytes 6291464 | tf_op jit(solution)/shard_map/ppermute | solution.py:54
  461.5 26.1 %collective-permute-start.40 = (bf16[2048,256]{1,0:T(8,128)(2,1)S(1)}, bf16[2048,256]{1,0:T(8,128)(2,1)S(1)}, u32[]{:S(2)}, u32[]{:S(2)}) collective-permute-start(bf16[2048,256]{1,0:T(8,128)(2,1)S(1)} %copy-done.30), channel_id=1, source_target_pairs={{0,2},{1,3},{2,0},{3,1},{4,6},{5,7},{6,4},{7,5},{8,10},{9,11},{10,... | collective-permute-start | bytes 3145736 | tf_op jit(solution)/shard_map/ppermute | solution.py:73
  463.8 26.1 %collective-permute-start.42 = (bf16[2048,256]{1,0:T(8,128)(2,1)S(1)}, bf16[2048,256]{1,0:T(8,128)(2,1)S(1)}, u32[]{:S(2)}, u32[]{:S(2)}) collective-permute-start(bf16[2048,256]{1,0:T(8,128)(2,1)S(1)} %fusion.24), channel_id=1, source_target_pairs={{0,1},{1,0},{2,3},{3,2},{4,5},{5,4},{6,7},{7,6},{8,9},{9,8},{10,11... | collective-permute-start | bytes 3145736 | tf_op jit(solution)/shard_map/ppermute | solution.py:73
  470.3 131.8 %collective-permute-start.50 = (bf16[256,2048]{1,0:T(8,128)(2,1)}, bf16[256,2048]{1,0:T(8,128)(2,1)}, u32[]{:S(2)}, u32[]{:S(2)}) collective-permute-start(bf16[256,2048]{1,0:T(8,128)(2,1)} %fusion.21), channel_id=1, source_target_pairs={{0,2},{1,3},{2,0},{3,1},{4,6},{5,7},{6,4},{7,5},{8,10},{9,11},{10,... | collective-permute-start | bytes 3145736 | tf_op jit(solution)/shard_map/ppermute | solution.py:83
  471.9 260.5 %collective-permute-start.49 = (bf16[256,2048]{1,0:T(8,128)(2,1)}, bf16[256,2048]{1,0:T(8,128)(2,1)}, u32[]{:S(2)}, u32[]{:S(2)}) collective-permute-start(bf16[256,2048]{1,0:T(8,128)(2,1)} %fusion.21), channel_id=1, source_target_pairs={{0,1},{1,0},{2,3},{3,2},{4,5},{5,4},{6,7},{7,6},{8,9},{9,8},{10,11... | collective-permute-start | bytes 3145736 | tf_op jit(solution)/shard_map/ppermute | solution.py:83
  487.6 19.9 %collective-permute-start.21 = (bf16[128,2048]{1,0:T(8,128)(2,1)}, bf16[128,2048]{1,0:T(8,128)(2,1)}, u32[]{:S(2)}, u32[]{:S(2)}) collective-permute-start(bf16[128,2048]{1,0:T(8,128)(2,1)} %get-tuple-element.54), channel_id=1, source_target_pairs={{0,8},{4,12},{8,16},{12,20},{16,24},{20,28},{24,0},{28,4},{1,9},{5... | collective-permute-start | bytes 1572872 | tf_op jit(solution)/shard_map/ppermute | solution.py:59
  489.9 41.6 %collective-permute-start.20 = (bf16[128,2048]{1,0:T(8,128)(2,1)}, bf16[128,2048]{1,0:T(8,128)(2,1)}, u32[]{:S(2)}, u32[]{:S(2)}) collective-permute-start(bf16[128,2048]{1,0:T(8,128)(2,1)} %get-tuple-element.55), channel_id=1, source_target_pairs={{0,16},{4,20},{8,24},{12,28},{16,0},{20,4},{24,8},{28,12},{1,17},{... | collective-permute-start | bytes 1572872 | tf_op jit(solution)/shard_map/ppermute | solution.py:59
  495.6 107.4 %all-to-all-start.4 = ((bf16[8,256,256]{2,1,0:T(8,128)(2,1)}), bf16[8,256,256]{2,1,0:T(8,128)(2,1)}, u32[]{:S(2)}, u32[]{:S(2)}) async-start(bf16[8,256,256]{2,1,0:T(8,128)(2,1)} %bitcast.58), calls=%async_computation.4 | async-start | bytes 2097152 | tf_op jit(solution)/shard_map/all_to_all | solution.py:98
  499.8 226.5 %all-reduce.2.cloned.1.call-start = ((), (), s32[]{:S(2)}) async-start(), calls=%async_computation.5 | async-start | bytes 163840 | tf_op jit(solution)/shard_map/psum | solution.py:341
  499.9 55.9 %copy-start.4 = (bf16[1,128,2048]{2,1,0:T(8,128)(2,1)S(1)}, bf16[1,128,2048]{2,1,0:T(8,128)(2,1)}, u32[]{:S(2)}) copy-start(bf16[1,128,2048]{2,1,0:T(8,128)(2,1)} %param.12) | copy-start | bytes 1572868
  499.9 55.9 %copy-start.25 = (f32[128]{0:T(128)S(1)}, f32[128]{0:T(128)}, u32[]{:S(2)}) copy-start(f32[128]{0:T(128)} %copy-done.24) | copy-start | bytes 1540
  499.9 55.9 %copy-start.29 = (f32[128]{0:T(128)S(1)}, f32[128]{0:T(128)}, u32[]{:S(2)}) copy-start(f32[128]{0:T(128)} %add_rsqrt_fusion.1) | copy-start | bytes 1540
  499.9 46.8 %collective-permute-start.19 = (bf16[128,2048]{1,0:T(8,128)(2,1)S(1)}, bf16[128,2048]{1,0:T(8,128)(2,1)S(1)}, u32[]{:S(2)}, u32[]{:S(2)}) collective-permute-start(bf16[128,2048]{1,0:T(8,128)(2,1)S(1)} %get-tuple-element.53), channel_id=1, source_target_pairs={{0,24},{4,28},{8,0},{12,4},{16,8},{20,12},{24,16},{28,20},{1,25},{... | collective-permute-start | bytes 1572872 | tf_op jit(solution)/shard_map/ppermute | solution.py:59
  507.4 91.3 %copy-start.23 = (f32[2048,1]{0,1:T(1,128)S(1)}, f32[2048,1]{0,1:T(1,128)}, u32[]{:S(2)}) copy-start(f32[2048,1]{0,1:T(1,128)} %slice_add_fusion.4) | copy-start | bytes 24580
  507.5 51.3 %collective-permute-start.17 = (bf16[128,2048]{1,0:T(8,128)(2,1)S(1)}, bf16[128,2048]{1,0:T(8,128)(2,1)S(1)}, u32[]{:S(2)}, u32[]{:S(2)}) collective-permute-start(bf16[128,2048]{1,0:T(8,128)(2,1)S(1)} %get-tuple-element.57), channel_id=1, source_target_pairs={{0,8},{4,12},{8,16},{12,20},{16,24},{20,28},{24,0},{28,4},{1,9},{5... | collective-permute-start | bytes 1572872 | tf_op jit(solution)/shard_map/ppermute | solution.py:59
  531.5 56.1 %collective-permute-start.16 = (bf16[128,2048]{1,0:T(8,128)(2,1)S(1)}, bf16[128,2048]{1,0:T(8,128)(2,1)S(1)}, u32[]{:S(2)}, u32[]{:S(2)}) collective-permute-start(bf16[128,2048]{1,0:T(8,128)(2,1)S(1)} %get-tuple-element.58), channel_id=1, source_target_pairs={{0,16},{4,20},{8,24},{12,28},{16,0},{20,4},{24,8},{28,12},{1,17},{... | collective-permute-start | bytes 1572872 | tf_op jit(solution)/shard_map/ppermute | solution.py:59
  546.8 51.9 %collective-permute-start.15 = (bf16[128,2048]{1,0:T(8,128)(2,1)S(1)}, bf16[128,2048]{1,0:T(8,128)(2,1)S(1)}, u32[]{:S(2)}, u32[]{:S(2)}) collective-permute-start(bf16[128,2048]{1,0:T(8,128)(2,1)S(1)} %get-tuple-element.56), channel_id=1, source_target_pairs={{0,24},{4,28},{8,0},{12,4},{16,8},{20,12},{24,16},{28,20},{1,25},{... | collective-permute-start | bytes 1572872 | tf_op jit(solution)/shard_map/ppermute | solution.py:59
  602.2 130.2 %collective-permute-start.51 = (bf16[256,2048]{1,0:T(8,128)(2,1)}, bf16[256,2048]{1,0:T(8,128)(2,1)S(1)}, u32[]{:S(2)}, u32[]{:S(2)}) collective-permute-start(bf16[256,2048]{1,0:T(8,128)(2,1)} %collective-permute-done.50), channel_id=1, source_target_pairs={{0,1},{1,0},{2,3},{3,2},{4,5},{5,4},{6,7},{7,6},{8,9},{9,8},{10,11... | collective-permute-start | bytes 3145736 | tf_op jit(solution)/shard_map/ppermute | solution.py:83
  603.0 128.8 %collective-permute-start.43 = (bf16[8,256,256]{2,1,0:T(8,128)(2,1)}, bf16[8,256,256]{2,1,0:T(8,128)(2,1)}, u32[]{:S(2)}, u32[]{:S(2)}) collective-permute-start(bf16[8,256,256]{2,1,0:T(8,128)(2,1)} %all-to-all-done.4), channel_id=1, source_target_pairs={{0,1},{1,0},{2,3},{3,2},{4,5},{5,4},{6,7},{7,6},{8,9},{9,8},{10,11... | collective-permute-start | bytes 3145736 | tf_op jit(solution)/shard_map/ppermute | solution.py:83
  727.7 80.2 %copy-start.26 = (f32[256]{0:T(256)}, f32[256]{0:T(256)S(1)}, u32[]{:S(2)}) copy-start(f32[256]{0:T(256)S(1)} %get-tuple-element.125) | copy-start | bytes 3076
  730.3 26.2 %collective-permute-start.44 = (bf16[8,256,256]{2,1,0:T(8,128)(2,1)}, bf16[8,256,256]{2,1,0:T(8,128)(2,1)S(1)}, u32[]{:S(2)}, u32[]{:S(2)}) collective-permute-start(bf16[8,256,256]{2,1,0:T(8,128)(2,1)} %all-to-all-done.4), channel_id=1, source_target_pairs={{0,2},{1,3},{2,0},{3,1},{4,6},{5,7},{6,4},{7,5},{8,10},{9,11},{10,... | collective-permute-start | bytes 3145736 | tf_op jit(solution)/shard_map/ppermute | solution.py:83
  731.8 46.9 %collective-permute-start.45 = (bf16[8,256,256]{2,1,0:T(8,128)(2,1)}, bf16[8,256,256]{2,1,0:T(8,128)(2,1)S(1)}, u32[]{:S(2)}, u32[]{:S(2)}) collective-permute-start(bf16[8,256,256]{2,1,0:T(8,128)(2,1)} %collective-permute-done.43), channel_id=1, source_target_pairs={{0,2},{1,3},{2,0},{3,1},{4,6},{5,7},{6,4},{7,5},{8,10},{9,11},{10,... | collective-permute-start | bytes 3145736 | tf_op jit(solution)/shard_map/ppermute | solution.py:83
  (34 other events, 558.3 us)
Sparse Core Ops, SparseCore 0:
  608.9 117.3 all-reduce.1

commit v2 on v1

v2 whole, which is shorter than its diff:
```python
import functools

import jax
import jax.numpy as jnp
import numpy as np
from jax import lax
from jax.experimental import pallas as pl
from jax.experimental.pallas import tpu as pltpu
from jax.sharding import PartitionSpec as P

D = 2048
H = 32
HD = 64
ROT = 32
FF = 8192

EPSILON = 1e-05
ROPE_BASE = 10000.0
MASK_VALUE = -1e30
F32 = jnp.float32
BF16 = jnp.bfloat16
GELU_C = 0.7978845608028654
HUGE = 2**38
MEDIUM = 2**27


def dot(left, right, contract=(1, 0)):
    return lax.dot_general(
        left, right, (((contract[0],), (contract[1],)), ((), ())), preferred_element_type=F32
    )


def flip(count, mask):
    return [(i, i ^ mask) for i in range(count)]


def replica_order(bits):
    count = lax.axis_size("replica")
    return sorted(range(count), key=lambda p: [p >> b & 1 for b in bits])


def cross(pair, bit, *hold):
    keep, send = pair
    got = lax.ppermute(send, "replica", flip(lax.axis_size("replica"), 1 << bit))
    return keep, after(got, *hold)


def last_pairs(pairs, orders, *hold):
    out = []
    for pair, bits in zip(pairs, orders):
        for bit in bits[1:-1]:
            pair = add([cross(pair, bit, *hold)])
        out.append(cross(pair, bits[-1], *hold))
    return out


def gather_replicas(piece, bits, *hold):
    count = lax.axis_size("replica")
    held = [piece]
    for b in bits[::-1]:
        got = [lax.ppermute(a, "replica", flip(count, 1 << b)) for a in held]
        held = held + [after(a, *hold) for a in got]
    return held


def spread_replicas(piece):
    count = lax.axis_size("replica")
    return [piece] + [lax.ppermute(piece, "replica", flip(count, p)) for p in range(1, count)]


def exchange(blocks):
    return lax.all_to_all(blocks, "shard", 0, 0, tiled=True)


def after(value, *others):
    return lax.optimization_barrier((value,) + others)[0]


def kernel_call(kernel, *, out_shape, cost=1, **options):
    def in_hbm(array):
        big = array.size * array.dtype.itemsize >= 2**18
        return pltpu.with_memory_space_constraint(array, pltpu.HBM) if big else array

    several = isinstance(out_shape, tuple)
    shapes = [
        pltpu.HBM(a.shape, a.dtype) if a.size * a.dtype.itemsize >= 2**18 else a
        for a in (out_shape if several else (out_shape,))
    ]
    call = pl.pallas_call(
        kernel,
        out_shape=tuple(shapes) if several else shapes[0],
        cost_estimate=pl.CostEstimate(flops=cost, bytes_accessed=cost, transcendentals=0),
        **options,
    )
    return lambda *args: call(*map(in_hbm, args))


def scalar(value):
    return jnp.reshape(value, (1,)).astype(jnp.int32)


def add(pairs, cost=1):
    n, columns = pairs[0][0].shape[0], pairs[0][0].shape[2]
    heights = [left.shape[1] for left, _ in pairs]
    half, rows = max(n // 2, 1), sum(heights)
    block = columns // 2 if columns % 256 == 0 else columns

    def kernel(*refs):
        ins, outs = refs[: 2 * len(pairs)], refs[2 * len(pairs) :]
        at = 0
        for j, height in enumerate(heights):
            for i in range(n):
                total = ins[2 * j][i].astype(F32) + ins[2 * j + 1][i].astype(F32)
                outs[i // half][i % half, at : at + height, :] = total.astype(BF16)
            at += height

    out = jax.ShapeDtypeStruct((half, rows, columns), BF16)
    return kernel_call(
        kernel,
        out_shape=(out,) * (n // half),
        grid=(columns // block,),
        in_specs=[
            pl.BlockSpec((n, height, block), lambda i: (0, 0, i)) for height in heights for _ in "12"
        ],
        out_specs=[pl.BlockSpec((half, rows, block), lambda i: (0, 0, i))] * (n // half),
        compiler_params=pltpu.CompilerParams(vmem_limit_bytes=40 * 2**20),
        cost=cost,
        name="add",
    )(*[x for pair in pairs for x in pair])


def select_rows(weight, replica, count, copies, groups):
    rows, width = weight.shape[0] // copies, weight.shape[1] // (groups * count)
    lanes = width if groups == 1 else 2 * HD

    def kernel(at, weight_ref, out):
        for i in range(count):
            for h in range(width // lanes):
                for g in range(groups):
                    here, to = (g * count + i) * width + h * lanes, (h * groups + g) * lanes
                    out[i, :, to : to + lanes] = weight_ref[:, here : here + lanes]

    shape = (count, rows, groups * width)
    return kernel_call(
        kernel,
        out_shape=jax.ShapeDtypeStruct(shape, weight.dtype),
        grid_spec=pltpu.PrefetchScalarGridSpec(
            num_scalar_prefetch=1,
            grid=(1,),
            in_specs=[pl.BlockSpec((rows, weight.shape[1]), lambda i, at: (at[0], 0))],
            out_specs=pl.BlockSpec(shape, lambda i, at: (0, 0, 0)),
        ),
        name="select_rows",
    )(scalar(replica), weight)


def join_weight(pieces, bits, replica):
    count, rows, columns = pieces[0].shape
    copies = len(pieces)

    def kernel(at, *refs):
        for p in range(copies):
            q = pl.multiple_of((at[0] ^ p) * rows, rows)
            refs[-1][0, pl.ds(q, rows), :] = refs[p][0]

    return kernel_call(
        kernel,
        out_shape=jax.ShapeDtypeStruct((count, copies * rows, columns), pieces[0].dtype),
        grid_spec=pltpu.PrefetchScalarGridSpec(
            num_scalar_prefetch=1,
            grid=(count,),
            in_specs=[pl.BlockSpec((1, rows, columns), lambda i, at: (i, 0, 0))] * copies,
            out_specs=pl.BlockSpec((1, copies * rows, columns), lambda i, at: (i, 0, 0)),
        ),
        name="join_weight",
    )(scalar(replica), *pieces).reshape(count * copies * rows, columns)


def join_rows(pieces, heights, bits, replica):
    rows, columns = pieces[0].shape
    copies, order, block = len(pieces), replica_order(bits), min(512, columns)
    steps = columns // block

    def kernel(at, *refs):
        outs, start = refs[copies:], 0
        for out, height in zip(outs, heights):
            for side in range(2):

                @pl.when(pl.program_id(0) == side)
                def _():
                    for p, ref in zip(order, refs):
                        q = pl.multiple_of((at[0] ^ p) * height, height)
                        at_row = start + side * height
                        out[pl.ds(q, height), :] = ref[at_row : at_row + height, :].astype(F32)

            start += 2 * height

    return kernel_call(
        kernel,
        out_shape=tuple(jax.ShapeDtypeStruct((copies * h, 2 * columns), F32) for h in heights),
        grid_spec=pltpu.PrefetchScalarGridSpec(
            num_scalar_prefetch=1,
            grid=(2, steps),
            in_specs=[pl.BlockSpec((rows, block), lambda s, i, at: (0, i))] * copies,
            out_specs=[
                pl.BlockSpec((copies * h, block), lambda s, i, at: (0, s * steps + i))
                for h in heights
            ],
        ),
        compiler_params=pltpu.CompilerParams(vmem_limit_bytes=40 * 2**20),
        name="join_rows",
    )(scalar(replica), *pieces)


def join_grad(pieces, bits, replica, groups, cost=1):
    count, rows, columns = pieces[0].shape
    copies, width = len(pieces), columns // groups
    order = replica_order(bits)
    lanes = width if groups == 1 else 2 * HD
    halves = width // lanes
    if groups == 1:
        grid, batch = (count, 1), 1
        ins = pl.BlockSpec((1, rows, width), lambda i, h, at: (i, 0, 0))
        out = pl.BlockSpec((copies * rows, width), lambda i, h, at: (0, i))
    else:
        grid, batch = (groups, halves), count
        ins = pl.BlockSpec((count, rows, lanes), lambda g, h, at: (0, 0, h * groups + g))
        out = pl.BlockSpec((copies * rows, count * width), lambda g, h, at: (0, g))

    def kernel(at, *refs):
        for h in range(halves):

            @pl.when(pl.program_id(1) == h)
            def _():
                for p, ref in zip(order, refs):
                    q = pl.ds(pl.multiple_of((at[0] ^ p) * rows, rows), rows)
                    for i in range(batch):
                        to = i * width + h * lanes
                        refs[-1][q, to : to + lanes] = ref[i].astype(F32)

    return kernel_call(
        kernel,
        out_shape=jax.ShapeDtypeStruct((copies * rows, groups * count * width), F32),
        grid_spec=pltpu.PrefetchScalarGridSpec(
            num_scalar_prefetch=1, grid=grid, in_specs=[ins] * copies, out_specs=out
        ),
        cost=cost,
        name="join_grad",
    )(scalar(replica), *pieces)


def norm_tokens(gathered, shard, rows, width):
    count = gathered.shape[0]
    lanes = 2 * HD

    def kernel(shard_ref, x_ref, small_ref,
               out_ref, gain_ref, shift_ref, bias_ref, attn_ref, all_ref):
        @pl.when(pl.program_id(0) == 0)
        def _():
            for b in range(count):
                row = small_ref[b].astype(F32)[:1]
                at = pl.ds(b * width, width)
                gain_ref[:, at] = row[:, :width]
                shift_ref[:, at] = row[:, width : 2 * width]
                bias_ref[:, at] = row[:, 5 * width : 6 * width] + row[:, 6 * width : 7 * width]
                all_ref[:, b * 3 * width : (b + 1) * 3 * width] = row[:, 2 * width : 5 * width]
            for t in range(3):
                for h in range(width // lanes):
                    at = pl.multiple_of(t * D + shard_ref[0] * width + h * lanes, lanes)
                    to = (h * 3 + t) * lanes
                    attn_ref[:, to : to + lanes] = all_ref[:, pl.ds(at, lanes)]

        xhat, _ = normalize(x_ref[0].astype(F32))
        out_ref[...] = (xhat * gain_ref[...] + shift_ref[...]).astype(BF16)

    once = pl.BlockSpec((1, D), lambda j, shard: (0, 0))
    vector = jax.ShapeDtypeStruct((1, D), F32)
    tokens = jax.ShapeDtypeStruct((count * rows, D), BF16)
    return kernel_call(
        kernel,
        out_shape=(tokens, vector, vector, vector, jax.ShapeDtypeStruct((1, 3 * width), F32)),
        grid_spec=pltpu.PrefetchScalarGridSpec(
            num_scalar_prefetch=1,
            grid=(count,),
            in_specs=[
                pl.BlockSpec((1, rows, D), lambda j, shard: (j, 0, 0)),
                pl.BlockSpec((count, 16, D), lambda j, shard: (0, 2 * rows // 16, 0)),
            ],
            out_specs=[pl.BlockSpec((rows, D), lambda j, shard: (j, 0))]
            + [once] * 3
            + [pl.BlockSpec((1, 3 * width), lambda j, shard: (0, 0))],
            scratch_shapes=[pltpu.VMEM((1, 3 * D), F32)],
        ),
        name="norm_tokens",
    )(scalar(shard), gathered, gathered)


def weight_grad(tokens, grads, replica, first, count, copies, bits):
    size, columns = grads.shape
    width = tokens.shape[1] // lax.axis_size("shard")
    rows = width // copies
    order = replica_order(bits)

    def kernel(at, left, right, keep, send, whole):
        whole[...] = dot(left[...], right[...], (0, 0)).astype(BF16)
        for i, p in enumerate(order):
            piece = whole[pl.ds(pl.multiple_of((at[0] ^ p) * rows, rows), rows), :]
            (keep, send)[i // (copies // 2)][i % (copies // 2)] = piece

    out = pl.BlockSpec((copies // 2, rows, columns), lambda s, at: (0, s, 0))
    return kernel_call(
        kernel,
        out_shape=(jax.ShapeDtypeStruct((copies // 2, count * rows, columns), BF16),) * 2,
        grid_spec=pltpu.PrefetchScalarGridSpec(
            num_scalar_prefetch=1,
            grid=(count,),
            in_specs=[
                pl.BlockSpec((size, width), lambda s, at: (0, first + s)),
                pl.BlockSpec((size, columns), lambda s, at: (0, 0)),
            ],
            out_specs=[out] * 2,
            scratch_shapes=[pltpu.VMEM((width, columns), BF16)],
        ),
        compiler_params=pltpu.CompilerParams(vmem_limit_bytes=40 * 2**20),
        name="weight_grad",
    )(scalar(replica), tokens, grads)


def cotangent_spec(gathered, columns=D, buffered=1):
    shape = (gathered.shape[0], gathered.shape[1] // 2 // 16 * 16, columns)
    return pl.BlockSpec(shape, lambda i, *at: (0, 1, 0), pipeline_mode=pl.Buffered(buffered))


def flat(ref):
    shape = ref.shape
    return ref[...].reshape(shape[0] * shape[1], shape[2])


def row_grad(left, gathered, replica, copies, orders):
    size, rows = left.shape
    part, half = rows // copies, copies // 2
    places = [replica_order(bits) for bits in orders]
    steps = copies if part % 128 == 0 else 1
    height = part if len(orders) == 2 else 2 * part

    def kernel(at, left, right, *refs):
        outs, whole = refs[:-1], refs[-1]

        def put(p, piece):
            for h in range(2):
                order, to = (places * 2)[h], (2 * h if len(orders) == 2 else 0)
                i, top = order.index(p), h * part if len(orders) == 1 else 0
                columns = piece[:, h * D // 2 : (h + 1) * D // 2]
                outs[to + i // half][i % half, top : top + part] = columns

        product = dot(left[...], flat(right), (0, 0)).astype(BF16)
        if steps == 1:
            whole[...] = product
            for p in range(copies):
                put(p, whole[pl.ds(pl.multiple_of((at[0] ^ p) * part, part), part), :])
            return
        for p in range(copies):
            pl.when(pl.program_id(0) == p)(functools.partial(put, p, product))

    shape = (half, height, D // 2)
    return kernel_call(
        kernel,
        out_shape=(jax.ShapeDtypeStruct(shape, BF16),) * (2 * len(orders)),
        grid_spec=pltpu.PrefetchScalarGridSpec(
            num_scalar_prefetch=1,
            grid=(steps,),
            in_specs=[
                pl.BlockSpec((size, rows // steps), lambda i, at: (0, (at[0] ^ i) % steps)),
                cotangent_spec(gathered),
            ],
            out_specs=[pl.BlockSpec(shape, lambda i, at: (0, 0, 0))] * (2 * len(orders)),
            scratch_shapes=[pltpu.VMEM((rows if steps == 1 else 16, D), BF16)],
        ),
        compiler_params=pltpu.CompilerParams(vmem_limit_bytes=48 * 2**20),
        name="row_grad",
    )(scalar(replica), left, gathered)


def feed_forward(normed, gathered, up, down, bias):
    size, ff = normed.shape[0], up.shape[1]
    block = 256
    step, parts = size // (size // 512), size // 512
    shards = gathered.shape[0] // parts

    def kernel(x, g, u, d, b, hidden, grad, total):
        total[...] = jnp.zeros_like(total)
        for i in range(parts):
            at = pl.ds(i * step, step)
            value, slope = gelu_and_slope(dot(x[at, :], u[...]) + b[...])
            hidden[at, :] = value.astype(BF16)
            up_to = g[i * shards : (i + 1) * shards].reshape(step, D)
            low = (dot(up_to, d[...], (1, 1)) * slope).astype(BF16)
            grad[at, :] = low
            total[...] += jnp.sum(low.astype(F32), axis=0, keepdims=True)

    whole = pl.BlockSpec((size, D), lambda f: (0, 0), pipeline_mode=pl.Buffered(1))
    column = pl.BlockSpec((size, block), lambda f: (0, f))
    vector = pl.BlockSpec((1, block), lambda f: (0, f))
    shape = jax.ShapeDtypeStruct((size, ff), BF16)
    return kernel_call(
        kernel,
        out_shape=(shape, shape, jax.ShapeDtypeStruct((1, ff), F32)),
        grid=(ff // block,),
        in_specs=[
            whole,
            cotangent_spec(gathered),
            pl.BlockSpec((D, block), lambda f: (0, f)),
            pl.BlockSpec((block, D), lambda f: (f, 0)),
            vector,
        ],
        out_specs=[column, column, vector],
        compiler_params=pltpu.CompilerParams(vmem_limit_bytes=50 * 2**20),
        name="feed_forward",
    )(normed, gathered, up, down, bias)


def project(normed, gathered, pieces, bias, dense, replica):
    count, rows, columns = pieces[0].shape
    copies, size, width = len(pieces), normed.shape[0], dense.shape[0]
    step = size // count

    def kernel(at, x, g, d, b, *refs):
        weight, out, grad = refs[copies:]

        @pl.when(pl.program_id(0) == 0)
        def _():
            for i in range(count):
                for p in range(copies):
                    q = pl.multiple_of((i * copies + (at[0] ^ p)) * rows, rows)
                    weight[pl.ds(q, rows), :] = refs[p][i]

        out[...] = dot(x[...], weight[...]) + b[...]
        grad[...] = dot(flat(g), d[...], (1, 1)).astype(BF16)

    def once(shape):
        zeros = (0,) * len(shape)
        return pl.BlockSpec(shape, lambda i, at: zeros, pipeline_mode=pl.Buffered(1))

    pair = 2
    tokens = gathered.shape[1] // 2 // 16 * 16
    return kernel_call(
        kernel,
        out_shape=(
            jax.ShapeDtypeStruct((D, columns), BF16),
            jax.ShapeDtypeStruct((size, columns), F32),
            jax.ShapeDtypeStruct((size, width), BF16),
        ),
        grid_spec=pltpu.PrefetchScalarGridSpec(
            num_scalar_prefetch=1,
            grid=(count // pair,),
            in_specs=[
                pl.BlockSpec((pair * step, D), lambda i, at: (i, 0)),
                pl.BlockSpec((pair, tokens, D), lambda i, at: (i, 1, 0)),
                once((width, D)),
                once((1, columns)),
            ]
            + [once((count, rows, columns))] * copies,
            out_specs=[
                once((D, columns)),
                pl.BlockSpec((pair * step, columns), lambda i, at: (i, 0)),
                pl.BlockSpec((pair * step, width), lambda i, at: (i, 0)),
            ],
        ),
        compiler_params=pltpu.CompilerParams(vmem_limit_bytes=40 * 2**20),
        name="project",
    )(scalar(replica), normed, gathered, dense, bias, *pieces)


def token_products(grad_projected, attn, grad_pre, up, hidden, down, mixed, dense):
    size = grad_pre.shape[0]
    step = min(256, size)

    def kernel(ga, wa, gu, wu, h, wd, m, wo, out):
        out[:, :D] = (
            dot(ga[...], wa[...], (1, 1)) + dot(gu[...], wu[...], (1, 1))
        ).astype(BF16)
        out[:, D:] = (dot(h[...], wd[...]) + dot(m[...], wo[...])).astype(BF16)

    def part(array):
        return pl.BlockSpec((step, array.shape[1]), lambda i: (i, 0))

    def whole(array):
        return pl.BlockSpec(array.shape, lambda i: (0, 0), pipeline_mode=pl.Buffered(1))

    args = (grad_projected, attn, grad_pre, up, hidden, down, mixed, dense)
    return kernel_call(
        kernel,
        out_shape=jax.ShapeDtypeStruct((size, 2 * D), BF16),
        grid=(size // step,),
        in_specs=[(part, whole)[i % 2](array) for i, array in enumerate(args)],
        out_specs=pl.BlockSpec((step, 2 * D), lambda i: (i, 0)),
        compiler_params=pltpu.CompilerParams(vmem_limit_bytes=48 * 2**20),
        cost=HUGE,
        name="token_products",
    )(*args)


def attention_kernel(
    q_ref, k_ref, v_ref, g_ref, cos_ref, lo_ref, hi_ref,
    mix_ref, grad_ref, sum_ref,
    q_sc, k_sc, v_sc, dk_sc, dv_sc,
    *, tokens, step,
):
    scale = HD**-0.5
    lanes = 2 * HD

    def turn(x, at, sign):
        cos, lo, hi = cos_ref[at, :], lo_ref[at, :], hi_ref[at, :]
        up = pltpu.roll(x, lanes - ROT // 2, 1)
        down = pltpu.roll(x, ROT // 2, 1)
        return x * cos + sign * (up * lo + down * hi)

    blocks = [pl.ds(i * step, step) for i in range(tokens // step)]
    for at in blocks:
        q_sc[at, :] = turn(q_ref[at, :], at, 1.0).astype(BF16)
        k_sc[at, :] = turn(k_ref[at, :], at, 1.0).astype(BF16)
        v_sc[at, :] = v_ref[at, :].astype(BF16)
    dk_sc[...] = jnp.zeros_like(dk_sc)
    dv_sc[...] = jnp.zeros_like(dv_sc)
    lane = lax.broadcasted_iota(jnp.int32, (1, lanes), 1)
    heads = [lane < HD, lane >= HD]
    for i, rows in enumerate(blocks):
        width = (i + 1) * step
        q, g = q_sc[rows, :], g_ref[rows, :]
        k, v = k_sc[:width, :], v_sc[:width, :]
        seen = lax.broadcasted_iota(jnp.int32, (step, width), 1) <= i * step + (
            lax.broadcasted_iota(jnp.int32, (step, width), 0)
        )
        mixed = jnp.zeros((step, lanes), F32)
        dq = jnp.zeros((step, lanes), F32)
        for mine in heads:
            zero = jnp.zeros((), BF16)
            qh, gh = jnp.where(mine, q, zero), jnp.where(mine, g, zero)
            scores = dot(qh, k, (1, 1)) * scale
            scores = jnp.where(seen, scores, MASK_VALUE)
            top = jnp.max(scores, axis=1, keepdims=True)
            raised = jnp.exp(scores - top)
            probs = raised / jnp.sum(raised, axis=1, keepdims=True)
            weights = probs.astype(BF16)
            mixed = jnp.where(mine, dot(weights, v), mixed)
            grad_probs = dot(gh, v, (1, 1))
            delta = jnp.sum(probs * grad_probs, axis=1, keepdims=True)
            grad_scores = (probs * (grad_probs - delta)).astype(BF16)
            dq = jnp.where(mine, dot(grad_scores, k), dq)
            dk_sc[:width, :] += dot(grad_scores, qh, (0, 0))
            dv_sc[:width, :] += dot(weights, gh, (0, 0))
        mix_ref[rows, :] = mixed.astype(BF16)
        grad_ref[rows, :lanes] = turn(dq * scale, rows, -1.0).astype(BF16)
    for at in blocks:
        grad_ref[at, lanes : 2 * lanes] = turn(dk_sc[at, :] * scale, at, -1.0).astype(BF16)
        grad_ref[at, 2 * lanes :] = dv_sc[at, :].astype(BF16)
    sum_ref[...] = jnp.zeros_like(sum_ref)
    for at in blocks:
        sum_ref[...] += jnp.sum(grad_ref[at, :].astype(F32), axis=0, keepdims=True)


def rope_tables(tokens):
    half = ROT // 2
    frequencies = np.float32(ROPE_BASE) ** (-2.0 * np.arange(half, dtype=np.float32) / ROT)
    angles = np.arange(tokens, dtype=np.float32)[:, None] * frequencies.astype(np.float32)[None]
    cosine, sine = np.cos(angles.astype(np.float64)), np.sin(angles.astype(np.float64))
    none, rest = np.zeros_like(sine), np.zeros((tokens, HD - ROT))
    tables = ([cosine, cosine, rest + 1.0], [-sine, none, rest], [none, sine, rest])
    return [np.concatenate(t * 2, axis=1).astype(np.float32) for t in tables]


def attention(projected, grad_mixed):
    tokens, width = grad_mixed.shape
    lanes = 2 * HD

    def column(stride, offset):
        return pl.BlockSpec((tokens, lanes), lambda h: (0, stride * h + offset))

    whole = pl.BlockSpec((tokens, lanes), lambda h: (0, 0))
    return kernel_call(
        functools.partial(attention_kernel, tokens=tokens, step=min(256, tokens)),
        out_shape=(
            jax.ShapeDtypeStruct((tokens, width), BF16),
            jax.ShapeDtypeStruct((tokens, 3 * width), BF16),
            jax.ShapeDtypeStruct((1, 3 * width), F32),
        ),
        grid=(width // lanes,),
        in_specs=[column(3, 0), column(3, 1), column(3, 2), column(1, 0), whole, whole, whole],
        out_specs=[
            column(1, 0),
            pl.BlockSpec((tokens, 3 * lanes), lambda h: (0, h)),
            pl.BlockSpec((1, 3 * lanes), lambda h: (0, h)),
        ],
        scratch_shapes=[pltpu.VMEM((tokens, lanes), BF16)] * 3
        + [pltpu.VMEM((tokens, lanes), F32)] * 2,
        compiler_params=pltpu.CompilerParams(vmem_limit_bytes=48 * 2**20),
        name="attention",
    )(projected, projected, projected, grad_mixed, *map(jnp.asarray, rope_tables(tokens)))


def group_sums(sums, groups):
    lanes, columns = 2 * HD, sums.shape[1]
    parts = columns // groups // lanes

    def kernel(ref, out):
        for h in range(parts):
            for g in range(groups):
                to, at = (g * parts + h) * lanes, (h * groups + g) * lanes
                out[:, to : to + lanes] = ref[:, at : at + lanes]

    return kernel_call(
        kernel, out_shape=jax.ShapeDtypeStruct(sums.shape, F32), cost=MEDIUM, name="group_sums"
    )(sums)


def finish(own, upstream, part, gain, out_bias, sum_attn, shard, count):
    width = D // count

    def kernel(at, x_ref, g_ref, part_ref, gain_ref, bias_ref, attn_ref, out, grad, sums):
        inputs, cotangent = x_ref[...].astype(F32), g_ref[...].astype(F32)
        out[...] = (inputs + part_ref[:, D:].astype(F32) + bias_ref[...]).astype(BF16)
        rows = part_ref[:, :D].astype(F32)
        xhat, inverse = normalize(inputs)
        scaled = rows * gain_ref[...]
        mean = jnp.mean(scaled, axis=-1, keepdims=True)
        along = jnp.mean(scaled * xhat, axis=-1, keepdims=True)
        grad[...] = (cotangent + inverse * (scaled - mean - xhat * along)).astype(BF16)
        for i, term in enumerate((rows * xhat, rows, cotangent)):
            total = jnp.sum(term, axis=0, keepdims=True)
            for j in range(count):
                sums[j : j + 1, i * width : (i + 1) * width] = total[:, j * width : (j + 1) * width]
        for slot in range(3):
            block = 3 * lax.broadcasted_iota(jnp.int32, (count, width), 0) + slot
            here = jnp.zeros((count, width), F32)
            for t in range(3):
                term = attn_ref[:, t * width : (t + 1) * width]
                here = jnp.where(block == t * count + at[0], term, here)
            sums[:, (3 + slot) * width : (4 + slot) * width] = here

    tokens = jax.ShapeDtypeStruct(own.shape, BF16)
    vmem = pl.BlockSpec(memory_space=pltpu.VMEM)
    return kernel_call(
        kernel,
        out_shape=(tokens, tokens, jax.ShapeDtypeStruct((count, 6 * width), F32)),
        in_specs=[pl.BlockSpec(memory_space=pltpu.SMEM)] + [vmem] * 6,
        out_specs=[vmem] * 3,
        compiler_params=pltpu.CompilerParams(vmem_limit_bytes=40 * 2**20),
        name="finish",
    )(scalar(shard), own, upstream, part, gain, out_bias, sum_attn)


def normalize(values):
    center = values - jnp.mean(values, axis=-1, keepdims=True)
    spread = jnp.mean(center * center, axis=-1, keepdims=True)
    inverse = lax.rsqrt(spread + EPSILON)
    return center * inverse, inverse


def gelu_and_slope(u):
    inner = GELU_C * (u + 0.044715 * u * u * u)
    t = jnp.tanh(inner)
    slope = 0.5 * (1.0 + t) + 0.5 * u * (1.0 - t * t) * GELU_C * (1.0 + 3 * 0.044715 * u * u)
    return 0.5 * u * (1.0 + t), slope


def shards(
    block_in,
    norm_gain,
    norm_bias,
    attn_weight,
    attn_bias,
    dense_weight,
    dense_bias,
    up_weight,
    up_bias,
    down_weight,
    down_bias,
    cotangent,
):
    own, upstream = block_in[0], cotangent[0]
    tok_rows = own.shape[0]
    count, copies = lax.axis_size("shard"), lax.axis_size("replica")
    shard, replica = lax.axis_index("shard"), lax.axis_index("replica")
    width = attn_weight.shape[0]
    ff = down_weight.shape[0]
    part_rows = width // copies
    bits = list(range(copies.bit_length() - 1))
    back = bits[::-1]

    small = jnp.concatenate(
        [norm_gain, norm_bias, attn_bias, dense_bias, down_bias, jnp.zeros((D - 7 * width,), BF16)]
    )
    packed = jnp.concatenate([own, upstream, jnp.broadcast_to(small[None], (16, D))], axis=0)
    up_part = exchange(select_rows(up_weight, replica, count, copies, 1))
    gathered = lax.all_gather(after(packed, up_part), "shard", axis=0)
    attn_part = exchange(after(select_rows(attn_weight, replica, count, copies, 3), up_part))
    up_mine = join_weight(spread_replicas(up_part), bits, replica)
    attn_pieces = spread_replicas(after(attn_part, up_mine))
    gathered = after(gathered, up_mine, *attn_pieces)
    normed, gain, shift, out_bias, attn_bias_mine = norm_tokens(gathered, shard, tok_rows, width)

    hidden, grad_pre, sum_up = feed_forward(
        normed, gathered, up_mine, down_weight, up_bias.astype(F32)[None]
    )
    half, orders = count // 2, (bits, back)

    def split(kernel_outs):
        return list(kernel_outs[:2]), list(kernel_outs[2:])

    def two_halves(grads):
        first = weight_grad(normed, grads, replica, 0, half, copies, bits)
        second = weight_grad(normed, after(grads, *first), replica, half, half, copies, back)
        return [first, second]

    def cross_both(pairs, *hold):
        return [cross(pair, order[0], *hold) for pair, order in zip(pairs, orders)]

    up_pairs = two_halves(grad_pre)
    down_pairs = split(
        row_grad(after(hidden, *up_pairs[1]), gathered, replica, copies, orders)
    )

    attn_mine, projected, grad_mixed = project(
        after(normed, *down_pairs[1]), gathered, attn_pieces, attn_bias_mine, dense_weight, replica
    )
    up_pairs = [add([terms]) for terms in cross_both(up_pairs, projected)]
    projected = after(projected, *up_pairs[0], *up_pairs[1])
    mixed, grad_projected, sum_attn = attention(projected, grad_mixed)
    dense_pair = row_grad(mixed, gathered, replica, copies, (back,))
    (grad_up,) = add(last_pairs(up_pairs, orders, *dense_pair))
    grad_up = grad_up.reshape(count, part_rows, ff)
    attn_pairs = two_halves(after(grad_projected, grad_up))
    grad_up = exchange(grad_up)

    rest = after(grad_projected, *attn_pairs[1])
    part = token_products(
        rest, attn_mine, grad_pre, up_mine, hidden, down_weight, mixed, dense_weight
    )
    own_part = lax.psum_scatter(part, "shard", scatter_dimension=0, tiled=True)
    grad_up = after(grad_up, part)

    first, second = cross_both(down_pairs, part, grad_up)
    rows_pairs = [add([first], HUGE), add([second, cross(dense_pair, back[0], part)])]
    attn_pairs = [add([terms]) for terms in cross_both(attn_pairs, *rows_pairs[1])]
    (grad_rows,) = add(last_pairs(rows_pairs, orders, *attn_pairs[1]))
    grad_rows = grad_rows[0]
    (grad_attn,) = add(last_pairs(attn_pairs, orders, grad_rows), MEDIUM)
    grad_attn = grad_attn.reshape(count, part_rows, 3 * width)
    sum_attn = group_sums(after(sum_attn, grad_attn), 3)
    grad_attn = after(exchange(grad_attn), sum_attn)
    up_pieces = gather_replicas(grad_up, bits)
    row_pieces = gather_replicas(grad_rows, back)
    down_whole, dense_whole = join_rows(row_pieces, (ff // copies, part_rows), back, replica)

    block_out, grad_in, sums = finish(
        own, upstream, after(own_part, grad_attn), gain, out_bias, sum_attn, shard, count
    )

    sums = jnp.sum(exchange(sums), axis=0)
    sums = sum(spread_replicas(jnp.concatenate([sums, sum_up[0]])))
    grad_out_bias = sums[2 * width : 3 * width]
    attn_pieces = gather_replicas(grad_attn, bits, grad_in)
    up_whole = join_grad([after(a, down_whole) for a in up_pieces], bits, replica, 1)
    attn_whole = join_grad([after(a, up_whole) for a in attn_pieces], bits, replica, 3)
    return (
        block_out[None],
        grad_in[None],
        sums[:width],
        sums[width : 2 * width],
        attn_whole,
        sums[3 * width : 6 * width],
        dense_whole,
        grad_out_bias,
        up_whole,
        sums[6 * width :],
        down_whole,
        grad_out_bias,
    )


def solution(mesh):
    vector, matrix = P("shard"), P("shard", None)
    rows = P("replica", "shard", None)
    return jax.shard_map(
        shards,
        mesh=mesh,
        in_specs=(rows, vector, vector, matrix, vector, matrix, vector, matrix, vector, matrix, vector, rows),
        out_specs=(rows, rows, vector, vector, matrix, vector, matrix, vector, matrix, vector, matrix, vector),
        check_vma=False,
    )
```

time: 823 us -> 469 us (0.57)
  Pallas kernels: 20.6 us -> 175 us
  waiting for transfers between devices: 312 us -> 203 us
  local copies, waits for them, and re-layouts: 119 us -> 10.3 us
  matrix products: 86.5 us -> 0 us
  blocking collectives: 91.5 us -> 10.9 us
  other arithmetic: 63 us -> 1.13 us
  starting transfers between devices: 108 us -> 52.2 us
    pallas_call x1 -> x28, Pallas kernels: 20.6 us -> 175 us  [kernel_call(): return lambda *args: call(*map(in_hbm, args))]
    all_gather x1 -> x0, blocking collectives: 91.5 us -> none  [shards(): small = lax.all_gather(packed, 'shard', axis=0, tiled=True).astype(F32)]
    dot_general x18 -> x0, matrix products: 86.5 us -> none  [dot(): lax.dot_general(left, right, (((contract[0],), (contract[1],)), ((), ()))...]
    psum x1 -> x0, waiting for transfers between devices: 85.6 us -> none  [shards(): sums = lax.psum(sums, ('shard', 'replica'))]
    ppermute x52 -> x31, waiting for transfers between devices: 215 us -> 140 us  [the longest x9 79.2 us: spread_replicas(): lax.ppermute(piece, 'replica', flip(count, p))]
    ppermute x52 -> x31, starting transfers between devices: 84 us -> 32.9 us  [the longest x13 14.6 us: cross(): lax.ppermute(send, 'replica', flip(lax.axis_size('replica'), 1 << bit))]
    convert_element_type x5 -> x0, local copies, waits for them, and re-layouts: 50.7 us -> none  [the longest x3 27.8 us: shards(): attn_whole.reshape(width, 3 * D).astype(F32)]
    all_to_all x5 -> x4, waiting for transfers between devices: 11.7 us -> 55.5 us  [exchange(): return lax.all_to_all(blocks, 'shard', 0, 0, tiled=True)]
  transfers between devices with their start and end apart: 58 -> 37, of which waited for: 25 -> 17; matrix products, arithmetic and copies ran while one was open for 29% -> 1% of each run, Pallas kernels for 3% -> 27%
where the time goes in v2:
time: 469 us; the launch traced here: 468 us
  waiting for transfers between devices  203 us (43%)
  Pallas kernels  175 us (37%)
  starting transfers between devices  52.2 us (11%)
  between operations  14.3 us (3%)
  blocking collectives  10.9 us (2%)
  local copies, waits for them, and re-layouts  10.3 us (2%)
    pallas_call x28, Pallas kernels, kernel_call(): return lambda *args: call(*map(in_hbm, args))  175 us
    ppermute x9, waiting for transfers between devices, spread_replicas(): lax.ppermute(piece, 'replica', flip(count, p))  79.2 us
    all_to_all x4, waiting for transfers between devices, exchange(): return lax.all_to_all(blocks, 'shard', 0, 0, tiled=True)  55.5 us
    ppermute x9, waiting for transfers between devices, gather_replicas(): got = [lax.ppermute(a, 'replica', flip(count, 1 << b)) for a in held]  43.3 us
    all_to_all x4, starting transfers between devices, exchange(): return lax.all_to_all(blocks, 'shard', 0, 0, tiled=True)  19.2 us
    ppermute x13, waiting for transfers between devices, cross(): lax.ppermute(send, 'replica', flip(lax.axis_size('replica'), 1 << bit))  17.6 us
    ppermute x13, starting transfers between devices, cross(): lax.ppermute(send, 'replica', flip(lax.axis_size('replica'), 1 << bit))  14.6 us
    all_to_all x1, blocking collectives, exchange(): return lax.all_to_all(blocks, 'shard', 0, 0, tiled=True)  10.9 us
  transfers between devices with their start and end apart: 37, of which 17 were waited for; matrix products, arithmetic and copies ran while one was open for 1% of the time, Pallas kernels for 27%

profile of v2, /device:TPU:0, one launch (start us, length us, event | category | flops | bytes accessed | tf_op | source)
XLA Modules:
  0.0 467.6 jit_solution(3590453675609735547)
XLA Ops:
  7.2 2.3 select_rows.2
  9.5 6.5 %all-to-all-start = ((bf16[8,64,1024]{2,1,0:T(8,128)(2,1)}), bf16[8,64,1024]{2,1,0:T(8,128)(2,1)S(1)}, u32[]{:S(2)}, u32[]{:S(2)}) async-start(bf16[8,64,1024]{2,1,0:T(8,128)(2,1)} %select_rows.2), calls=%async_computation | async-start | bytes 2097152 | tf_op jit(solution)/shard_map/all_to_all | solution.py:72
  17.4 1.1 pad_maximum_fusion
  18.4 24.1 %all-to-all-done.refs_0_ = bf16[8,64,1024]{2,1,0:T(8,128)(2,1)S(1)} async-done(((bf16[8,64,1024]{2,1,0:T(8,128)(2,1)}), bf16[8,64,1024]{2,1,0:T(8,128)(2,1)S(1)}, u32[]{:S(2)}, u32[]{:S(2)}) %all-to-all-start) | async-done | bytes 1048608 | tf_op jit(solution)/shard_map/all_to_all | solution.py:72
  42.6 2.6 select_rows.3
  45.2 3.6 all-to-all-start.1
  48.7 2.5 collective-permute-start.2
  52.3 23.4 %collective-permute-done.2.refs_3_ = bf16[8,64,1024]{2,1,0:T(8,128)(2,1)S(1)} collective-permute-done((bf16[8,64,1024]{2,1,0:T(8,128)(2,1)S(1)}, bf16[8,64,1024]{2,1,0:T(8,128)(2,1)S(1)}, u32[]{:S(2)}, u32[]{:S(2)}) %collective-permute-start.2) | collective-permute-done | bytes 1048608 | tf_op jit(solution)/shard_map/ppermute | solution.py:68
  75.7 21.8 %collective-permute-done.1.refs_2_ = bf16[8,64,1024]{2,1,0:T(8,128)(2,1)S(1)} collective-permute-done((bf16[8,64,1024]{2,1,0:T(8,128)(2,1)S(1)}, bf16[8,64,1024]{2,1,0:T(8,128)(2,1)S(1)}, u32[]{:S(2)}, u32[]{:S(2)}) %collective-permute-start.1) | collective-permute-done | bytes 1048608 | tf_op jit(solution)/shard_map/ppermute | solution.py:68
  98.6 6.6 %join_weight.1 = bf16[8,256,1024]{2,1,0:T(8,128)(2,1)} custom-call(s32[1]{0:T(128)} %bitcast.3.at, bf16[8,64,1024]{2,1,0:T(8,128)(2,1)} %copy-done.6, bf16[8,64,1024]{2,1,0:T(8,128)(2,1)} %collective-permute-done.refs_1_, bf16[8,64,1024]{2,1,0:T(8,128)(2,1)} %copy-done.13, bf16[8,64,1024]{2,1,0:T(8,128)(2,1)} %copy-done.12), custom_call_target="tpu_custom_call" | custom-call | flops 1 | bytes 1 | tf_op jit(solution)/shard_map/join_weight/pallas_call | solution.py:95
  105.2 1.8 collective-permute-start.5
  107.0 1.2 collective-permute-start.4
  108.8 17.8 %collective-permute-done.5.refs_3_ = bf16[8,64,768]{2,1,0:T(8,128)(2,1)S(1)} collective-permute-done((bf16[8,64,768]{2,1,0:T(8,128)(2,1)S(1)}, bf16[8,64,768]{2,1,0:T(8,128)(2,1)S(1)}, u32[]{:S(2)}, u32[]{:S(2)}) %collective-permute-start.5) | collective-permute-done | bytes 786464 | tf_op jit(solution)/shard_map/ppermute | solution.py:68
  126.6 16.0 %collective-permute-done.4.refs_2_ = bf16[8,64,768]{2,1,0:T(8,128)(2,1)S(1)} collective-permute-done((bf16[8,64,768]{2,1,0:T(8,128)(2,1)S(1)}, bf16[8,64,768]{2,1,0:T(8,128)(2,1)S(1)}, u32[]{:S(2)}, u32[]{:S(2)}) %collective-permute-start.4) | collective-permute-done | bytes 786464 | tf_op jit(solution)/shard_map/ppermute | solution.py:68
  143.3 8.1 %norm_tokens.1 = (bf16[1024,2048]{1,0:T(8,128)(2,1)}, f32[1,2048]{1,0:T(1,128)}, f32[1,2048]{1,0:T(1,128)}, f32[1,2048]{1,0:T(1,128)}, f32[1,768]{1,0:T(1,128)}) custom-call(s32[1]{0:T(128)} %bitcast.shard_ref.at, bf16[8,272,2048]{2,1,0:T(8,128)(2,1)} %bitcast.18, bf16[8,272,2048]{2,1,0:T(8,128)(2,1)} %bitcast.19), custom_call_target="tpu_custom_call" | custom-call | flops 1 | bytes 1 | tf_op jit(solution)/shard_map/norm_tokens/pallas_call | solution.py:95
  151.4 17.0 %feed_forward.1 = (bf16[1024,1024]{1,0:T(8,128)(2,1)}, bf16[1024,1024]{1,0:T(8,128)(2,1)}, f32[1,1024]{1,0:T(1,128)S(1)}) custom-call(bf16[1024,2048]{1,0:T(8,128)(2,1)} %get-tuple-element.110.x.left, bf16[8,272,2048]{2,1,0:T(8,128)(2,1)} %bitcast.20, bf16[2048,1024]{1,0:T(8,128)(2,1)} %bitcast.24, bf16[1024,2048]{1,0:T(8,128)(2,1)} %wd.1, ...), custom_call_target="tpu_custom_call" | custom-call | flops 1 | bytes 1 | tf_op jit(solution)/shard_map/feed_forward/pallas_call | solution.py:95
  168.4 6.2 %weight_grad.4 = (bf16[2,256,1024]{2,1,0:T(8,128)(2,1)}, bf16[2,256,1024]{2,1,0:T(8,128)(2,1)}) custom-call(s32[1]{0:T(128)} %bitcast.3.at, bf16[1024,2048]{1,0:T(8,128)(2,1)} %get-tuple-element.110.x.left, bf16[1024,1024]{1,0:T(8,128)(2,1)} %get-tuple-element.104.right.gu), custom_call_target="tpu_custom_call" | custom-call | flops 1 | bytes 1 | tf_op jit(solution)/shard_map/weight_grad/pallas_call | solution.py:95
  174.6 6.3 %weight_grad.5 = (bf16[2,256,1024]{2,1,0:T(8,128)(2,1)}, bf16[2,256,1024]{2,1,0:T(8,128)(2,1)}) custom-call(s32[1]{0:T(128)} %bitcast.3.at, bf16[1024,2048]{1,0:T(8,128)(2,1)} %get-tuple-element.110.x.left, bf16[1024,1024]{1,0:T(8,128)(2,1)} %get-tuple-element.104.right.gu), custom_call_target="tpu_custom_call" | custom-call | flops 1 | bytes 1 | tf_op jit(solution)/shard_map/weight_grad/pallas_call | solution.py:95
  181.0 1.5 collective-permute-start.7
  182.5 1.5 collective-permute-start.6
  184.0 10.0 %row_grad.2 = (bf16[2,256,1024]{2,1,0:T(8,128)(2,1)}, bf16[2,256,1024]{2,1,0:T(8,128)(2,1)}, bf16[2,256,1024]{2,1,0:T(8,128)(2,1)}, bf16[2,256,1024]{2,1,0:T(8,128)(2,1)}) custom-call(s32[1]{0:T(128)} %bitcast.3.at, bf16[1024,1024]{1,0:T(8,128)(2,1)} %get-tuple-element.107.left.h, bf16[8,272,2048]{2,1,0:T(8,128)(2,1)} %bitcast.21), custom_call_target="tpu_custom_call" | custom-call | flops 1 | bytes 1 | tf_op jit(solution)/shard_map/row_grad/pallas_call | solution.py:95
  194.0 10.1 %project.1 = (bf16[2048,768]{1,0:T(8,128)(2,1)}, f32[1024,768]{1,0:T(8,128)}, bf16[1024,256]{1,0:T(8,128)(2,1)}) custom-call(s32[1]{0:T(128)} %bitcast.3.at, bf16[1024,2048]{1,0:T(8,128)(2,1)} %get-tuple-element.110.x.left, bf16[8,272,2048]{2,1,0:T(8,128)(2,1)} %bitcast.22, bf16[256,2048]{1,0:T(8,128)(2,1)} %wo.1, f32[1,768]{1,0:T(1,128)S(1)} %copy-done.3, ...), custom_call_target="tpu_custom_call" | custom-call | flops 1 | bytes 1 | tf_op jit(solution)/shard_map/project/pallas_call | solution.py:95
  204.1 2.4 collective-permute-done.7.refs_1_
  206.5 1.0 collective-permute-done.6.refs_1_
  208.5 2.4 add.27
  211.5 2.4 add.28
  213.9 1.5 collective-permute-start.9
  215.4 1.5 collective-permute-start.11
  217.4 21.2 %attention.1 = (bf16[1024,256]{1,0:T(8,128)(2,1)}, bf16[1024,768]{1,0:T(8,128)(2,1)}, f32[1,768]{1,0:T(1,128)S(1)}) custom-call(f32[1024,768]{1,0:T(8,128)} %get-tuple-element.119.q_ref.k_ref.v_ref, f32[1024,768]{1,0:T(8,128)} %get-tuple-element.119.q_ref.k_ref.v_ref, f32[1024,768]{1,0:T(8,128)} %get-tuple-element.119.q_ref.k_ref.v_ref, ...), custom_call_target="tpu_custom_call" | custom-call | flops 1 | bytes 1 | tf_op jit(solution)/shard_map/attention/pallas_call | solution.py:95
  239.2 4.7 row_grad.3
  246.0 2.5 add.29
  248.5 4.4 all-to-all-start.2
  253.0 5.8 %weight_grad.6 = (bf16[2,256,768]{2,1,0:T(8,128)(2,1)}, bf16[2,256,768]{2,1,0:T(8,128)(2,1)}) custom-call(s32[1]{0:T(128)} %bitcast.3.at, bf16[1024,2048]{1,0:T(8,128)(2,1)} %get-tuple-element.110.x.left, bf16[1024,768]{1,0:T(8,128)(2,1)} %get-tuple-element.133.right.ga), custom_call_target="tpu_custom_call" | custom-call | flops 1 | bytes 1 | tf_op jit(solution)/shard_map/weight_grad/pallas_call | solution.py:95
  258.7 1.4 collective-permute-start.10
  260.2 5.6 %weight_grad.7 = (bf16[2,256,768]{2,1,0:T(8,128)(2,1)}, bf16[2,256,768]{2,1,0:T(8,128)(2,1)}) custom-call(s32[1]{0:T(128)} %bitcast.3.at, bf16[1024,2048]{1,0:T(8,128)(2,1)} %get-tuple-element.110.x.left, bf16[1024,768]{1,0:T(8,128)(2,1)} %get-tuple-element.133.right.ga), custom_call_target="tpu_custom_call" | custom-call | flops 1 | bytes 1 | tf_op jit(solution)/shard_map/weight_grad/pallas_call | solution.py:95
  265.7 1.3 collective-permute-start.16
  267.1 20.4 %token_products.1 = bf16[1024,4096]{1,0:T(8,128)(2,1)} custom-call(bf16[1024,768]{1,0:T(8,128)(2,1)} %get-tuple-element.133.right.ga, bf16[2048,768]{1,0:T(8,128)(2,1)} %get-tuple-element.134.wa, bf16[1024,1024]{1,0:T(8,128)(2,1)} %get-tuple-element.104.right.gu, bf16[2048,1024]{1,0:T(8,128)(2,1)} %bitcast.25, bf16[1024,1024]{1,0:T(8,128)(2,1)} %get-tuple-element.107.left.h, ...), custom_call_target="tpu_custom_call" | custom-call | flops 274877906944 | bytes 274877906944 | tf_op jit(solution)/shard_map/token_products/pallas_call | solution.py:95
  287.6 2.9 add.30
  291.2 2.4 add.32
  294.1 2.2 add.33
  296.3 1.5 collective-permute-start.18
  297.8 2.2 add.31
  300.0 1.4 collective-permute-start.13
  301.4 7.2 %collective-permute-done.15.refs_1_ = bf16[1,256,1024]{2,1,0:T(8,128)(2,1)S(1)} collective-permute-done((bf16[1,256,1024]{2,1,0:T(8,128)(2,1)}, bf16[1,256,1024]{2,1,0:T(8,128)(2,1)S(1)}, u32[]{:S(2)}, u32[]{:S(2)}) %collective-permute-start.15) | collective-permute-done | bytes 524320 | tf_op jit(solution)/shard_map/ppermute | solution.py:44
  308.6 2.6 collective-permute-done.17.refs_3_
  311.2 2.7 add.34
  314.0 4.4 collective-permute-done.18.refs_3_
  319.2 2.3 add.35
  321.5 4.8 %all-to-all-start.3 = ((bf16[8,64,768]{2,1,0:T(8,128)(2,1)}), bf16[8,64,768]{2,1,0:T(8,128)(2,1)S(1)}, u32[]{:S(2)}, u32[]{:S(2)}) async-start(bf16[8,64,768]{2,1,0:T(8,128)(2,1)} %bitcast.30), calls=%async_computation.4 | async-start | bytes 1572864 | tf_op jit(solution)/shard_map/all_to_all | solution.py:72
  327.7 1.3 group_sums.1.attn_ref
  328.9 31.3 %all-to-all-done.3.refs_0_ = bf16[8,64,768]{2,1,0:T(8,128)(2,1)S(1)} async-done(((bf16[8,64,768]{2,1,0:T(8,128)(2,1)}), bf16[8,64,768]{2,1,0:T(8,128)(2,1)S(1)}, u32[]{:S(2)}, u32[]{:S(2)}) %all-to-all-start.3) | async-done | bytes 786464 | tf_op jit(solution)/shard_map/all_to_all | solution.py:72
  361.6 1.5 collective-permute-start.23
  363.6 1.5 collective-permute-start.27
  365.1 15.6 %collective-permute-done.28.refs_1_ = bf16[8,64,768]{2,1,0:T(8,128)(2,1)S(1)} collective-permute-done((bf16[8,64,768]{2,1,0:T(8,128)(2,1)S(1)}, bf16[8,64,768]{2,1,0:T(8,128)(2,1)S(1)}, u32[]{:S(2)}, u32[]{:S(2)}) %collective-permute-start.28) | collective-permute-done | bytes 786464 | tf_op jit(solution)/shard_map/ppermute | solution.py:61
  382.4 7.3 %reduce-scatter.2.cloned.1.call-done.part_ref = bf16[128,4096]{1,0:T(8,128)(2,1)} async-done(((bf16[1024,4096]{1,0:T(8,128)(2,1)}), bf16[128,4096]{1,0:T(8,128)(2,1)}) %reduce-scatter.2.cloned.1.call-update) | async-done | bytes 1048592 | tf_op jit(solution)/shard_map/reduce_scatter | solution.py:739
  390.3 3.4 finish.1
  393.8 1.5 collective-permute-start.30
  395.3 10.9 %all_to_all.29 = f32[8,1,1536]{2,1,0:T(1,128)S(1)} all-to-all(f32[8,1,1536]{2,1,0:T(1,128)S(1)} %copy.27), channel_id=1, replica_groups=mesh['shard'=8,'replica'=4] {'shard'}, dimensions={0} | all-to-all | bytes 98304 | tf_op jit(solution)/shard_map/all_to_all | solution.py:72
  406.3 3.6 collective-permute-done.27.refs_3_
  409.9 1.3 collective-permute-start.20
  411.9 24.1 %collective-permute-done.24.refs_3_ = bf16[640,1024]{1,0:T(8,128)(2,1)} collective-permute-done((bf16[640,1024]{1,0:T(8,128)(2,1)S(1)}, bf16[640,1024]{1,0:T(8,128)(2,1)}, u32[]{:S(2)}, u32[]{:S(2)}) %collective-permute-start.24) | collective-permute-done | bytes 1310752 | tf_op jit(solution)/shard_map/ppermute | solution.py:61
  436.8 8.1 %join_rows.1 = (f32[1024,2048]{1,0:T(8,128)}, f32[256,2048]{1,0:T(8,128)}) custom-call(s32[1]{0:T(128)} %bitcast.3.at, bf16[640,1024]{1,0:T(8,128)(2,1)} %bitcast.26, bf16[640,1024]{1,0:T(8,128)(2,1)} %copy-done.11, bf16[640,1024]{1,0:T(8,128)(2,1)} %collective-permute-done.23.refs_2_, bf16[640,1024]{1,0:T(8,128)(2,1)} %collective-permute-done.24.refs_3_), custom_call_target="tpu_custom_call" | custom-call | flops 1 | bytes 1 | tf_op jit(solution)/shard_map/join_rows/pallas_call | solution.py:95
  444.9 7.4 %join_grad.2 = f32[256,8192]{1,0:T(8,128)} custom-call(s32[1]{0:T(128)} %bitcast.3.at, bf16[8,64,1024]{2,1,0:T(8,128)(2,1)} %all-to-all-done.2.refs_0_, bf16[8,64,1024]{2,1,0:T(8,128)(2,1)} %collective-permute-done.25.refs_1_, bf16[8,64,1024]{2,1,0:T(8,128)(2,1)} %collective-permute-done.26.refs_2_, bf16[8,64,1024]{2,1,0:T(8,128)(2,1)} %collective-permute-done.27.refs_3_), custom_call_target="tpu_custom_call" | custom-call | flops 1 | bytes 1 | tf_op jit(solution)/shard_map/join_grad/pallas_call | solution.py:95
  454.1 6.1 %join_grad.3 = f32[256,6144]{1,0:T(8,128)} custom-call(s32[1]{0:T(128)} %bitcast.3.at, bf16[8,64,768]{2,1,0:T(8,128)(2,1)} %copy-done.8, bf16[8,64,768]{2,1,0:T(8,128)(2,1)} %copy-done.19, bf16[8,64,768]{2,1,0:T(8,128)(2,1)} %collective-permute-done.29.refs_2_, bf16[8,64,768]{2,1,0:T(8,128)(2,1)} %collective-permute-done.30.refs_3_), custom_call_target="tpu_custom_call" | custom-call | flops 1 | bytes 1 | tf_op jit(solution)/shard_map/join_grad/pallas_call | solution.py:95
  (126 shorter events, 21.3 us)
Async XLA Ops:
  7.2 8.9 %copy-start.28 = (bf16[256]{0:T(256)(128)(2,1)S(1)}, bf16[256]{0:T(256)(128)(2,1)}, u32[]{:S(2)}) copy-start(bf16[256]{0:T(256)(128)(2,1)} %param.16) | copy-start | bytes 1540
  7.2 9.1 %copy-start.29 = (bf16[256]{0:T(256)(128)(2,1)S(1)}, bf16[256]{0:T(256)(128)(2,1)}, u32[]{:S(2)}) copy-start(bf16[256]{0:T(256)(128)(2,1)} %param.17) | copy-start | bytes 1540
  7.2 9.3 %copy-start.27 = (bf16[768]{0:T(1024)(128)(2,1)S(1)}, bf16[768]{0:T(1024)(128)(2,1)}, u32[]{:S(2)}) copy-start(bf16[768]{0:T(1024)(128)(2,1)} %param.19) | copy-start | bytes 4612
  7.2 9.5 %copy-start.30 = (bf16[256]{0:T(256)(128)(2,1)S(1)}, bf16[256]{0:T(256)(128)(2,1)}, u32[]{:S(2)}) copy-start(bf16[256]{0:T(256)(128)(2,1)} %param.21) | copy-start | bytes 1540
  7.2 9.7 %copy-start.31 = (bf16[256]{0:T(256)(128)(2,1)S(1)}, bf16[256]{0:T(256)(128)(2,1)}, u32[]{:S(2)}) copy-start(bf16[256]{0:T(256)(128)(2,1)} %param.25) | copy-start | bytes 1540
  9.5 7.8 %copy-start.9 = (bf16[1,128,2048]{2,1,0:T(8,128)(2,1)S(1)}, bf16[1,128,2048]{2,1,0:T(8,128)(2,1)}, u32[]{:S(2)}) copy-start(bf16[1,128,2048]{2,1,0:T(8,128)(2,1)} %param.15) | copy-start | bytes 1572868
  9.5 7.8 %copy-start.10 = (bf16[1,128,2048]{2,1,0:T(8,128)(2,1)S(1)}, bf16[1,128,2048]{2,1,0:T(8,128)(2,1)}, u32[]{:S(2)}) copy-start(bf16[1,128,2048]{2,1,0:T(8,128)(2,1)} %param.26) | copy-start | bytes 1572868
  9.5 33.1 %all-to-all-start = ((bf16[8,64,1024]{2,1,0:T(8,128)(2,1)}), bf16[8,64,1024]{2,1,0:T(8,128)(2,1)S(1)}, u32[]{:S(2)}, u32[]{:S(2)}) async-start(bf16[8,64,1024]{2,1,0:T(8,128)(2,1)} %select_rows.2), calls=%async_computation | async-start | bytes 2097152 | tf_op jit(solution)/shard_map/all_to_all | solution.py:72
  16.0 127.3 %all-gather.3.cloned.1.call-start = ((), (), s32[]{:S(2)}) async-start(), calls=%async_computation.7 | async-start | bytes 10027008 | tf_op jit(solution)/shard_map/all_gather | solution.py:695
  42.6 9.2 %copy-start.6 = (bf16[8,64,1024]{2,1,0:T(8,128)(2,1)}, bf16[8,64,1024]{2,1,0:T(8,128)(2,1)S(1)}, u32[]{:S(2)}) copy-start(bf16[8,64,1024]{2,1,0:T(8,128)(2,1)S(1)} %all-to-all-done.refs_0_) | copy-start | bytes 3145732
  45.2 60.0 %all-to-all-start.1 = ((bf16[8,64,768]{2,1,0:T(8,128)(2,1)}), bf16[8,64,768]{2,1,0:T(8,128)(2,1)S(1)}, u32[]{:S(2)}, u32[]{:S(2)}) async-start(bf16[8,64,768]{2,1,0:T(8,128)(2,1)} %select_rows.3), calls=%async_computation.1 | async-start | bytes 1572864 | tf_op jit(solution)/shard_map/all_to_all | solution.py:72
  48.7 60.0 %copy-start.26 = (bf16[1024]{0:T(1024)(128)(2,1)S(1)}, bf16[1024]{0:T(1024)(128)(2,1)}, u32[]{:S(2)}) copy-start(bf16[1024]{0:T(1024)(128)(2,1)} %param.23) | copy-start | bytes 6148
  48.7 27.0 %collective-permute-start.2 = (bf16[8,64,1024]{2,1,0:T(8,128)(2,1)S(1)}, bf16[8,64,1024]{2,1,0:T(8,128)(2,1)S(1)}, u32[]{:S(2)}, u32[]{:S(2)}) collective-permute-start(bf16[8,64,1024]{2,1,0:T(8,128)(2,1)S(1)} %all-to-all-done.refs_0_), channel_id=1, source_target_pairs={{0,3},{1,2},{2,1},{3,0},{4,7},{5,6},{6,5},{7,4},{8,11},{9,10},{10,... | collective-permute-start | bytes 3145736 | tf_op jit(solution)/shard_map/ppermute | solution.py:68
  51.2 46.3 %collective-permute-start.1 = (bf16[8,64,1024]{2,1,0:T(8,128)(2,1)S(1)}, bf16[8,64,1024]{2,1,0:T(8,128)(2,1)S(1)}, u32[]{:S(2)}, u32[]{:S(2)}) collective-permute-start(bf16[8,64,1024]{2,1,0:T(8,128)(2,1)S(1)} %all-to-all-done.refs_0_), channel_id=1, source_target_pairs={{0,2},{1,3},{2,0},{3,1},{4,6},{5,7},{6,4},{7,5},{8,10},{9,11},{10,... | collective-permute-start | bytes 3145736 | tf_op jit(solution)/shard_map/ppermute | solution.py:68
  51.8 46.8 %collective-permute-start = (bf16[8,64,1024]{2,1,0:T(8,128)(2,1)S(1)}, bf16[8,64,1024]{2,1,0:T(8,128)(2,1)}, u32[]{:S(2)}, u32[]{:S(2)}) collective-permute-start(bf16[8,64,1024]{2,1,0:T(8,128)(2,1)S(1)} %all-to-all-done.refs_0_), channel_id=1, source_target_pairs={{0,1},{1,0},{2,3},{3,2},{4,5},{5,4},{6,7},{7,6},{8,9},{9,8},{10,11... | collective-permute-start | bytes 3145736 | tf_op jit(solution)/shard_map/ppermute | solution.py:68
  75.7 22.8 %copy-start.12 = (bf16[8,64,1024]{2,1,0:T(8,128)(2,1)}, bf16[8,64,1024]{2,1,0:T(8,128)(2,1)S(1)}, u32[]{:S(2)}) copy-start(bf16[8,64,1024]{2,1,0:T(8,128)(2,1)S(1)} %collective-permute-done.2.refs_3_) | copy-start | bytes 3145732
  97.6 1.0 copy-start.13
  105.2 46.2 %copy-start.7 = (bf16[8,64,768]{2,1,0:T(8,128)(2,1)}, bf16[8,64,768]{2,1,0:T(8,128)(2,1)S(1)}, u32[]{:S(2)}) copy-start(bf16[8,64,768]{2,1,0:T(8,128)(2,1)S(1)} %all-to-all-done.1.refs_0_) | copy-start | bytes 2359300
  105.2 21.4 %collective-permute-start.5 = (bf16[8,64,768]{2,1,0:T(8,128)(2,1)S(1)}, bf16[8,64,768]{2,1,0:T(8,128)(2,1)S(1)}, u32[]{:S(2)}, u32[]{:S(2)}) collective-permute-start(bf16[8,64,768]{2,1,0:T(8,128)(2,1)S(1)} %all-to-all-done.1.refs_0_), channel_id=1, source_target_pairs={{0,3},{1,2},{2,1},{3,0},{4,7},{5,6},{6,5},{7,4},{8,11},{9,10},{10,... | collective-permute-start | bytes 2359304 | tf_op jit(solution)/shard_map/ppermute | solution.py:68
  107.0 35.6 %collective-permute-start.4 = (bf16[8,64,768]{2,1,0:T(8,128)(2,1)S(1)}, bf16[8,64,768]{2,1,0:T(8,128)(2,1)S(1)}, u32[]{:S(2)}, u32[]{:S(2)}) collective-permute-start(bf16[8,64,768]{2,1,0:T(8,128)(2,1)S(1)} %all-to-all-done.1.refs_0_), channel_id=1, source_target_pairs={{0,2},{1,3},{2,0},{3,1},{4,6},{5,7},{6,4},{7,5},{8,10},{9,11},{10,... | collective-permute-start | bytes 2359304 | tf_op jit(solution)/shard_map/ppermute | solution.py:68
  108.2 34.5 %collective-permute-start.3 = (bf16[8,64,768]{2,1,0:T(8,128)(2,1)S(1)}, bf16[8,64,768]{2,1,0:T(8,128)(2,1)S(1)}, u32[]{:S(2)}, u32[]{:S(2)}) collective-permute-start(bf16[8,64,768]{2,1,0:T(8,128)(2,1)S(1)} %all-to-all-done.1.refs_0_), channel_id=1, source_target_pairs={{0,1},{1,0},{2,3},{3,2},{4,5},{5,4},{6,7},{7,6},{8,9},{9,8},{10,11... | collective-permute-start | bytes 2359304 | tf_op jit(solution)/shard_map/ppermute | solution.py:68
  126.6 24.8 %copy-start.16 = (bf16[8,64,768]{2,1,0:T(8,128)(2,1)}, bf16[8,64,768]{2,1,0:T(8,128)(2,1)S(1)}, u32[]{:S(2)}) copy-start(bf16[8,64,768]{2,1,0:T(8,128)(2,1)S(1)} %collective-permute-done.5.refs_3_) | copy-start | bytes 2359300
  142.6 8.8 %copy-start.17 = (bf16[8,64,768]{2,1,0:T(8,128)(2,1)}, bf16[8,64,768]{2,1,0:T(8,128)(2,1)S(1)}, u32[]{:S(2)}) copy-start(bf16[8,64,768]{2,1,0:T(8,128)(2,1)S(1)} %collective-permute-done.4.refs_2_) | copy-start | bytes 2359300
  142.7 8.7 %copy-start.18 = (bf16[8,64,768]{2,1,0:T(8,128)(2,1)}, bf16[8,64,768]{2,1,0:T(8,128)(2,1)S(1)}, u32[]{:S(2)}) copy-start(bf16[8,64,768]{2,1,0:T(8,128)(2,1)S(1)} %collective-permute-done.3.refs_1_) | copy-start | bytes 2359300
  174.6 7.9 %copy-start.32 = (bf16[2,256,1024]{2,1,0:T(8,128)(2,1)S(1)}, bf16[2,256,1024]{2,1,0:T(8,128)(2,1)}, u32[]{:S(2)}) copy-start(bf16[2,256,1024]{2,1,0:T(8,128)(2,1)} %get-tuple-element.103) | copy-start | bytes 3145732
  181.0 25.5 %collective-permute-start.7 = (bf16[2,256,1024]{2,1,0:T(8,128)(2,1)}, bf16[2,256,1024]{2,1,0:T(8,128)(2,1)S(1)}, u32[]{:S(2)}, u32[]{:S(2)}) collective-permute-start(bf16[2,256,1024]{2,1,0:T(8,128)(2,1)} %get-tuple-element.106), channel_id=1, source_target_pairs={{0,2},{1,3},{2,0},{3,1},{4,6},{5,7},{6,4},{7,5},{8,10},{9,11},{10,... | collective-permute-start | bytes 3145736 | tf_op jit(solution)/shard_map/ppermute | solution.py:44
  182.5 25.0 %collective-permute-start.6 = (bf16[2,256,1024]{2,1,0:T(8,128)(2,1)S(1)}, bf16[2,256,1024]{2,1,0:T(8,128)(2,1)S(1)}, u32[]{:S(2)}, u32[]{:S(2)}) collective-permute-start(bf16[2,256,1024]{2,1,0:T(8,128)(2,1)S(1)} %copy-done.32), channel_id=1, source_target_pairs={{0,1},{1,0},{2,3},{3,2},{4,5},{5,4},{6,7},{7,6},{8,9},{9,8},{10,11... | collective-permute-start | bytes 3145736 | tf_op jit(solution)/shard_map/ppermute | solution.py:44
  184.0 10.0 %copy-start.3 = (f32[1,768]{1,0:T(1,128)S(1)}, f32[1,768]{1,0:T(1,128)}, u32[]{:S(2)}) copy-start(f32[1,768]{1,0:T(1,128)} %get-tuple-element.111.b) | copy-start | bytes 9220
  206.5 5.0 %copy-start.14 = (bf16[2,256,1024]{2,1,0:T(8,128)(2,1)}, bf16[2,256,1024]{2,1,0:T(8,128)(2,1)S(1)}, u32[]{:S(2)}) copy-start(bf16[2,256,1024]{2,1,0:T(8,128)(2,1)S(1)} %collective-permute-done.7.refs_1_) | copy-start | bytes 3145732
  207.5 1.0 copy-start.15
  210.9 33.5 %collective-permute-start.8 = (bf16[1,256,1024]{2,1,0:T(8,128)(2,1)}, bf16[1,256,1024]{2,1,0:T(8,128)(2,1)S(1)}, u32[]{:S(2)}, u32[]{:S(2)}) collective-permute-start(bf16[1,256,1024]{2,1,0:T(8,128)(2,1)} %get-tuple-element.115), channel_id=1, source_target_pairs={{0,2},{1,3},{2,0},{3,1},{4,6},{5,7},{6,4},{7,5},{8,10},{9,11},{10,... | collective-permute-start | bytes 1572872 | tf_op jit(solution)/shard_map/ppermute | solution.py:44
  213.9 30.5 %collective-permute-start.9 = (bf16[1,256,1024]{2,1,0:T(8,128)(2,1)}, bf16[1,256,1024]{2,1,0:T(8,128)(2,1)S(1)}, u32[]{:S(2)}, u32[]{:S(2)}) collective-permute-start(bf16[1,256,1024]{2,1,0:T(8,128)(2,1)} %get-tuple-element.118), channel_id=1, source_target_pairs={{0,1},{1,0},{2,3},{3,2},{4,5},{5,4},{6,7},{7,6},{8,9},{9,8},{10,11... | collective-permute-start | bytes 1572872 | tf_op jit(solution)/shard_map/ppermute | solution.py:44
  215.4 72.2 %collective-permute-start.11 = (bf16[2,256,1024]{2,1,0:T(8,128)(2,1)}, bf16[2,256,1024]{2,1,0:T(8,128)(2,1)}, u32[]{:S(2)}, u32[]{:S(2)}) collective-permute-start(bf16[2,256,1024]{2,1,0:T(8,128)(2,1)} %get-tuple-element.109), channel_id=1, source_target_pairs={{0,2},{1,3},{2,0},{3,1},{4,6},{5,7},{6,4},{7,5},{8,10},{9,11},{10,... | collective-permute-start | bytes 3145736 | tf_op jit(solution)/shard_map/ppermute | solution.py:44
  216.9 70.7 %collective-permute-start.14 = (bf16[2,256,1024]{2,1,0:T(8,128)(2,1)}, bf16[2,256,1024]{2,1,0:T(8,128)(2,1)}, u32[]{:S(2)}, u32[]{:S(2)}) collective-permute-start(bf16[2,256,1024]{2,1,0:T(8,128)(2,1)} %get-tuple-element.144), channel_id=1, source_target_pairs={{0,1},{1,0},{2,3},{3,2},{4,5},{5,4},{6,7},{7,6},{8,9},{9,8},{10,11... | collective-permute-start | bytes 3145736 | tf_op jit(solution)/shard_map/ppermute | solution.py:44
  243.8 43.7 %collective-permute-start.12 = (bf16[2,128,1024]{2,1,0:T(8,128)(2,1)}, bf16[2,128,1024]{2,1,0:T(8,128)(2,1)}, u32[]{:S(2)}, u32[]{:S(2)}) collective-permute-start(bf16[2,128,1024]{2,1,0:T(8,128)(2,1)} %get-tuple-element.124), channel_id=1, source_target_pairs={{0,2},{1,3},{2,0},{3,1},{4,6},{5,7},{6,4},{7,5},{8,10},{9,11},{10,... | collective-permute-start | bytes 1572872 | tf_op jit(solution)/shard_map/ppermute | solution.py:44
  248.5 39.1 %all-to-all-start.2 = ((bf16[8,64,1024]{2,1,0:T(8,128)(2,1)}), bf16[8,64,1024]{2,1,0:T(8,128)(2,1)}, u32[]{:S(2)}, u32[]{:S(2)}) async-start(bf16[8,64,1024]{2,1,0:T(8,128)(2,1)} %bitcast.29), calls=%async_computation.3 | async-start | bytes 2097152 | tf_op jit(solution)/shard_map/all_to_all | solution.py:72
  252.9 136.7 %reduce-scatter.2.cloned.1.call-start = ((), (), s32[]{:S(2)}) async-start(), calls=%async_computation.6 | async-start | bytes 9437184 | tf_op jit(solution)/shard_map/reduce_scatter | solution.py:739
  258.7 39.1 %collective-permute-start.10 = (bf16[2,256,768]{2,1,0:T(8,128)(2,1)}, bf16[2,256,768]{2,1,0:T(8,128)(2,1)}, u32[]{:S(2)}, u32[]{:S(2)}) collective-permute-start(bf16[2,256,768]{2,1,0:T(8,128)(2,1)} %get-tuple-element.129), channel_id=1, source_target_pairs={{0,1},{1,0},{2,3},{3,2},{4,5},{5,4},{6,7},{7,6},{8,9},{9,8},{10,11... | collective-permute-start | bytes 2359304 | tf_op jit(solution)/shard_map/ppermute | solution.py:44
  265.7 28.3 %collective-permute-start.16 = (bf16[2,256,768]{2,1,0:T(8,128)(2,1)}, bf16[2,256,768]{2,1,0:T(8,128)(2,1)}, u32[]{:S(2)}, u32[]{:S(2)}) collective-permute-start(bf16[2,256,768]{2,1,0:T(8,128)(2,1)} %get-tuple-element.132), channel_id=1, source_target_pairs={{0,2},{1,3},{2,0},{3,1},{4,6},{5,7},{6,4},{7,5},{8,10},{9,11},{10,... | collective-permute-start | bytes 2359304 | tf_op jit(solution)/shard_map/ppermute | solution.py:44
  290.5 20.8 %collective-permute-start.17 = (bf16[1,384,1024]{2,1,0:T(8,128)(2,1)}, bf16[1,384,1024]{2,1,0:T(8,128)(2,1)}, u32[]{:S(2)}, u32[]{:S(2)}) collective-permute-start(bf16[1,384,1024]{2,1,0:T(8,128)(2,1)} %get-tuple-element.139), channel_id=1, source_target_pairs={{0,1},{1,0},{2,3},{3,2},{4,5},{5,4},{6,7},{7,6},{8,9},{9,8},{10,11... | collective-permute-start | bytes 2359304 | tf_op jit(solution)/shard_map/ppermute | solution.py:44
  293.5 15.1 %collective-permute-start.15 = (bf16[1,256,1024]{2,1,0:T(8,128)(2,1)}, bf16[1,256,1024]{2,1,0:T(8,128)(2,1)S(1)}, u32[]{:S(2)}, u32[]{:S(2)}) collective-permute-start(bf16[1,256,1024]{2,1,0:T(8,128)(2,1)} %get-tuple-element.147), channel_id=1, source_target_pairs={{0,2},{1,3},{2,0},{3,1},{4,6},{5,7},{6,4},{7,5},{8,10},{9,11},{10,... | collective-permute-start | bytes 1572872 | tf_op jit(solution)/shard_map/ppermute | solution.py:44
  296.3 22.0 %collective-permute-start.18 = (bf16[1,256,768]{2,1,0:T(8,128)(2,1)}, bf16[1,256,768]{2,1,0:T(8,128)(2,1)S(1)}, u32[]{:S(2)}, u32[]{:S(2)}) collective-permute-start(bf16[1,256,768]{2,1,0:T(8,128)(2,1)} %get-tuple-element.150), channel_id=1, source_target_pairs={{0,1},{1,0},{2,3},{3,2},{4,5},{5,4},{6,7},{7,6},{8,9},{9,8},{10,11... | collective-permute-start | bytes 1179656 | tf_op jit(solution)/shard_map/ppermute | solution.py:44
  300.0 18.3 %collective-permute-start.13 = (bf16[1,256,768]{2,1,0:T(8,128)(2,1)}, bf16[1,256,768]{2,1,0:T(8,128)(2,1)S(1)}, u32[]{:S(2)}, u32[]{:S(2)}) collective-permute-start(bf16[1,256,768]{2,1,0:T(8,128)(2,1)} %get-tuple-element.142), channel_id=1, source_target_pairs={{0,2},{1,3},{2,0},{3,1},{4,6},{5,7},{6,4},{7,5},{8,10},{9,11},{10,... | collective-permute-start | bytes 1179656 | tf_op jit(solution)/shard_map/ppermute | solution.py:44
  308.6 2.6 copy-start.20
  313.9 12.4 %copy-start.5 = (bf16[1,640,1024]{2,1,0:T(8,128)(2,1)S(1)}, bf16[1,640,1024]{2,1,0:T(8,128)(2,1)}, u32[]{:S(2)}) copy-start(bf16[1,640,1024]{2,1,0:T(8,128)(2,1)} %add.34) | copy-start | bytes 3932164
  313.9 75.7 %copy-start = (f32[1,2048]{1,0:T(1,128)S(1)}, f32[1,2048]{1,0:T(1,128)}, u32[]{:S(2)}) copy-start(f32[1,2048]{1,0:T(1,128)} %get-tuple-element.159.gain_ref) | copy-start | bytes 24580
  313.9 75.7 %copy-start.1 = (f32[1,2048]{1,0:T(1,128)S(1)}, f32[1,2048]{1,0:T(1,128)}, u32[]{:S(2)}) copy-start(f32[1,2048]{1,0:T(1,128)} %get-tuple-element.160.bias_ref) | copy-start | bytes 24580
  321.5 38.8 %all-to-all-start.3 = ((bf16[8,64,768]{2,1,0:T(8,128)(2,1)}), bf16[8,64,768]{2,1,0:T(8,128)(2,1)S(1)}, u32[]{:S(2)}, u32[]{:S(2)}) async-start(bf16[8,64,768]{2,1,0:T(8,128)(2,1)} %bitcast.30), calls=%async_computation.4 | async-start | bytes 1572864 | tf_op jit(solution)/shard_map/all_to_all | solution.py:72
  326.3 36.8 %collective-permute-start.22 = (bf16[640,1024]{1,0:T(8,128)(2,1)S(1)}, bf16[640,1024]{1,0:T(8,128)(2,1)S(1)}, u32[]{:S(2)}, u32[]{:S(2)}) collective-permute-start(bf16[640,1024]{1,0:T(8,128)(2,1)S(1)} %bitcast.27), channel_id=1, source_target_pairs={{0,1},{1,0},{2,3},{3,2},{4,5},{5,4},{6,7},{7,6},{8,9},{9,8},{10,11... | collective-permute-start | bytes 3932168 | tf_op jit(solution)/shard_map/ppermute | solution.py:61
  327.2 36.5 %collective-permute-start.25 = (bf16[8,64,1024]{2,1,0:T(8,128)(2,1)}, bf16[8,64,1024]{2,1,0:T(8,128)(2,1)}, u32[]{:S(2)}, u32[]{:S(2)}) collective-permute-start(bf16[8,64,1024]{2,1,0:T(8,128)(2,1)} %all-to-all-done.2.refs_0_), channel_id=1, source_target_pairs={{0,2},{1,3},{2,0},{3,1},{4,6},{5,7},{6,4},{7,5},{8,10},{9,11},{10,... | collective-permute-start | bytes 3145736 | tf_op jit(solution)/shard_map/ppermute | solution.py:61
  360.3 84.6 %copy-start.8 = (bf16[8,64,768]{2,1,0:T(8,128)(2,1)}, bf16[8,64,768]{2,1,0:T(8,128)(2,1)S(1)}, u32[]{:S(2)}) copy-start(bf16[8,64,768]{2,1,0:T(8,128)(2,1)S(1)} %all-to-all-done.3.refs_0_) | copy-start | bytes 2359300
  360.3 20.4 %collective-permute-start.28 = (bf16[8,64,768]{2,1,0:T(8,128)(2,1)S(1)}, bf16[8,64,768]{2,1,0:T(8,128)(2,1)S(1)}, u32[]{:S(2)}, u32[]{:S(2)}) collective-permute-start(bf16[8,64,768]{2,1,0:T(8,128)(2,1)S(1)} %all-to-all-done.3.refs_0_), channel_id=1, source_target_pairs={{0,2},{1,3},{2,0},{3,1},{4,6},{5,7},{6,4},{7,5},{8,10},{9,11},{10,... | collective-permute-start | bytes 2359304 | tf_op jit(solution)/shard_map/ppermute | solution.py:61
  361.0 32.7 %collective-permute-start.26 = (bf16[8,64,1024]{2,1,0:T(8,128)(2,1)}, bf16[8,64,1024]{2,1,0:T(8,128)(2,1)}, u32[]{:S(2)}, u32[]{:S(2)}) collective-permute-start(bf16[8,64,1024]{2,1,0:T(8,128)(2,1)} %all-to-all-done.2.refs_0_), channel_id=1, source_target_pairs={{0,1},{1,0},{2,3},{3,2},{4,5},{5,4},{6,7},{7,6},{8,9},{9,8},{10,11... | collective-permute-start | bytes 3145736 | tf_op jit(solution)/shard_map/ppermute | solution.py:61
  361.6 49.6 %collective-permute-start.23 = (bf16[640,1024]{1,0:T(8,128)(2,1)S(1)}, bf16[640,1024]{1,0:T(8,128)(2,1)}, u32[]{:S(2)}, u32[]{:S(2)}) collective-permute-start(bf16[640,1024]{1,0:T(8,128)(2,1)S(1)} %bitcast.28), channel_id=1, source_target_pairs={{0,2},{1,3},{2,0},{3,1},{4,6},{5,7},{6,4},{7,5},{8,10},{9,11},{10,... | collective-permute-start | bytes 3932168 | tf_op jit(solution)/shard_map/ppermute | solution.py:61
  363.1 73.7 %copy-start.11 = (bf16[640,1024]{1,0:T(8,128)(2,1)}, bf16[640,1024]{1,0:T(8,128)(2,1)S(1)}, u32[]{:S(2)}) copy-start(bf16[640,1024]{1,0:T(8,128)(2,1)S(1)} %collective-permute-done.22.refs_1_) | copy-start | bytes 3932164
  363.1 72.9 %collective-permute-start.24 = (bf16[640,1024]{1,0:T(8,128)(2,1)S(1)}, bf16[640,1024]{1,0:T(8,128)(2,1)}, u32[]{:S(2)}, u32[]{:S(2)}) collective-permute-start(bf16[640,1024]{1,0:T(8,128)(2,1)S(1)} %collective-permute-done.22.refs_1_), channel_id=1, source_target_pairs={{0,2},{1,3},{2,0},{3,1},{4,6},{5,7},{6,4},{7,5},{8,10},{9,11},{10,... | collective-permute-start | bytes 3932168 | tf_op jit(solution)/shard_map/ppermute | solution.py:61
  363.6 46.3 %collective-permute-start.27 = (bf16[8,64,1024]{2,1,0:T(8,128)(2,1)}, bf16[8,64,1024]{2,1,0:T(8,128)(2,1)}, u32[]{:S(2)}, u32[]{:S(2)}) collective-permute-start(bf16[8,64,1024]{2,1,0:T(8,128)(2,1)} %collective-permute-done.25.refs_1_), channel_id=1, source_target_pairs={{0,1},{1,0},{2,3},{3,2},{4,5},{5,4},{6,7},{7,6},{8,9},{9,8},{10,11... | collective-permute-start | bytes 3145736 | tf_op jit(solution)/shard_map/ppermute | solution.py:61
  380.7 0.9 copy-start.19
  381.6 70.7 %collective-permute-start.29 = (bf16[8,64,768]{2,1,0:T(8,128)(2,1)S(1)}, bf16[8,64,768]{2,1,0:T(8,128)(2,1)}, u32[]{:S(2)}, u32[]{:S(2)}) collective-permute-start(bf16[8,64,768]{2,1,0:T(8,128)(2,1)S(1)} %all-to-all-done.3.refs_0_), channel_id=1, source_target_pairs={{0,1},{1,0},{2,3},{3,2},{4,5},{5,4},{6,7},{7,6},{8,9},{9,8},{10,11... | collective-permute-start | bytes 2359304 | tf_op jit(solution)/shard_map/ppermute | solution.py:61
  393.8 60.4 %collective-permute-start.30 = (bf16[8,64,768]{2,1,0:T(8,128)(2,1)}, bf16[8,64,768]{2,1,0:T(8,128)(2,1)}, u32[]{:S(2)}, u32[]{:S(2)}) collective-permute-start(bf16[8,64,768]{2,1,0:T(8,128)(2,1)} %copy-done.19), channel_id=1, source_target_pairs={{0,1},{1,0},{2,3},{3,2},{4,5},{5,4},{6,7},{7,6},{8,9},{9,8},{10,11... | collective-permute-start | bytes 2359304 | tf_op jit(solution)/shard_map/ppermute | solution.py:61
  409.9 42.4 %collective-permute-start.20 = (f32[2560]{0:T(1024)S(1)}, f32[2560]{0:T(1024)S(1)}, u32[]{:S(2)}, u32[]{:S(2)}) collective-permute-start(f32[2560]{0:T(1024)S(1)} %pad_maximum_fusion.1), channel_id=1, source_target_pairs={{0,2},{1,3},{2,0},{3,1},{4,6},{5,7},{6,4},{7,5},{8,10},{9,11},{10,... | collective-permute-start | bytes 30728 | tf_op jit(solution)/shard_map/ppermute | solution.py:68
  411.2 41.1 %collective-permute-start.21 = (f32[2560]{0:T(1024)S(1)}, f32[2560]{0:T(1024)S(1)}, u32[]{:S(2)}, u32[]{:S(2)}) collective-permute-start(f32[2560]{0:T(1024)S(1)} %pad_maximum_fusion.1), channel_id=1, source_target_pairs={{0,3},{1,2},{2,1},{3,0},{4,7},{5,6},{6,5},{7,4},{8,11},{9,10},{10,... | collective-permute-start | bytes 30728 | tf_op jit(solution)/shard_map/ppermute | solution.py:68
  436.0 16.4 %collective-permute-start.19 = (f32[2560]{0:T(1024)S(1)}, f32[2560]{0:T(1024)S(1)}, u32[]{:S(2)}, u32[]{:S(2)}) collective-permute-start(f32[2560]{0:T(1024)S(1)} %pad_maximum_fusion.1), channel_id=1, source_target_pairs={{0,1},{1,0},{2,3},{3,2},{4,5},{5,4},{6,7},{7,6},{8,9},{9,8},{10,11... | collective-permute-start | bytes 30728 | tf_op jit(solution)/shard_map/ppermute | solution.py:68
  454.1 6.1 %copy-start.25 = (f32[256]{0:T(256)}, f32[256]{0:T(256)S(1)}, u32[]{:S(2)}) copy-start(f32[256]{0:T(256)S(1)} %get-tuple-element.204) | copy-start | bytes 3076
  (6 other events, 4.5 us)
Sparse Core Ops, SparseCore 0:
  42.7 100.5 all-gather.2
  287.7 101.9 reduce-scatter.1
